TPU v7x, 128 devices: a whole 4x4x4 slice. The times are simulated.
128 devices in a mesh: dev: 128 (over z, x, y, core).
Axes of the slice: x: 4, y: 4, z: 4, core: 2. Of those that a mesh axis runs over, the one named last changes fastest.
Arguments:
- grain_boxes: float32 [256, 64, 4096], P('dev'), may hold values from 0 to 1
- box_anchors: int32 [256, 3], P('dev'), may hold values from 0 to 127, as said below
- migrations: int32 [128, 2], P('dev'), may hold values from 0 to 1, as said below
Outputs:
- new_boxes: float32 [256, 64, 4096], P('dev')
Inputs may be any that keep to these rules, and one draw needn't show every extreme that they name: `box_anchors`: box b belongs to device d = b // 2; its first coordinate is d - 1, d or d + 1 modulo 128; the other two coordinates are 0 to 3. `migrations`: the two entries of a row differ, so each device hands exactly one box to each neighbour and receives one from each.
All inputs are finite; a program needn't handle non-finite values.
Results may differ from a plain program's by a relative error of at most 0.0003.
Values sent between devices are 32-bit elements; how exact they have to be, the bound alone decides.
No kernel may reach another device: no remote copies, remote signals or barrier semaphores. Data moves between devices by JAX's collectives and lax.ppermute only.
A program may use at most 128 MiB of HBM per device.

v0:
```python
import jax
import jax.numpy as jnp
from jax import lax
from jax.sharding import PartitionSpec as P

SUBSTEPS = 4


growth_rate = 1.0
quartic_rate = 1.0
coupling = 1.5
gradient_energy = 2.0
time_step = 0.02


def from_behind(value, axis, steps):
    count = lax.axis_size(axis)
    pairs = [(source, (source + steps) % count) for source in range(count)]
    return lax.ppermute(value, axis, pairs)


def laplacian_flat(order_field):
    box_edge = order_field.shape[1]
    area = order_field.shape[2]
    zeros_row = jnp.zeros_like(order_field[:, :1])
    upper_x = jnp.concatenate([order_field[:, 1:], zeros_row], axis=1)
    lower_x = jnp.concatenate([zeros_row, order_field[:, :-1]], axis=1)
    zeros_line = jnp.zeros_like(order_field[:, :, :box_edge])
    upper_y = jnp.concatenate([order_field[:, :, box_edge:], zeros_line], axis=2)
    lower_y = jnp.concatenate([zeros_line, order_field[:, :, :-box_edge]], axis=2)
    column = lax.broadcasted_iota(jnp.int32, (1, 1, area), 2) % box_edge
    zeros_cell = jnp.zeros_like(order_field[:, :, :1])
    upper_z = jnp.where(
        column == box_edge - 1, 0.0, jnp.concatenate([order_field[:, :, 1:], zeros_cell], axis=2)
    )
    lower_z = jnp.where(
        column == 0, 0.0, jnp.concatenate([zeros_cell, order_field[:, :, :-1]], axis=2)
    )
    beside = upper_x + lower_x + upper_y + lower_y + upper_z + lower_z
    return beside - 6.0 * order_field


def relax_steps(order_field, others):
    for substep in range(SUBSTEPS):
        driving = growth_rate * order_field - quartic_rate * order_field * order_field * order_field
        driving = (
            driving
            - 2.0 * coupling * order_field * others
            + gradient_energy * laplacian_flat(order_field)
        )
        order_field = order_field + time_step * driving
    return order_field


def shift_table(box_edge, tile_extent, offset):
    row_index = lax.broadcasted_iota(jnp.int32, (box_edge, tile_extent), 0)
    col_index = lax.broadcasted_iota(jnp.int32, (box_edge, tile_extent), 1)
    return (col_index == (row_index + offset) % tile_extent).astype(jnp.float32)


def place_square(square, anchor, half_edge):
    box_edge = square.shape[0]
    tile_extent = 2 * box_edge
    table_z = shift_table(box_edge, tile_extent, anchor[2] * half_edge)
    spread = jnp.dot(
        square.reshape(box_edge * box_edge, box_edge),
        table_z,
        precision=lax.Precision.HIGHEST,
        preferred_element_type=jnp.float32,
    )
    spread = spread.reshape(box_edge, box_edge, tile_extent)
    spread = jnp.pad(spread, ((0, 0), (0, tile_extent - box_edge), (0, 0)))
    return jnp.roll(spread, anchor[1] * half_edge, axis=1)


def extract_window(tile_sum, anchor, box_edge):
    half_edge = tile_sum.shape[0]
    tile_extent = tile_sum.shape[2]
    table_z = shift_table(box_edge, tile_extent, anchor[2] * half_edge)
    rolled = jnp.roll(tile_sum, -anchor[1] * half_edge, axis=1)[:, :box_edge, :]
    picked = jnp.dot(
        rolled.reshape(half_edge * box_edge, tile_extent),
        table_z.T,
        precision=lax.Precision.HIGHEST,
        preferred_element_type=jnp.float32,
    )
    return picked.reshape(half_edge, box_edge * box_edge)


def on_device(grain_boxes, box_anchors, migrations):
    box_count = grain_boxes.shape[0]
    box_edge = grain_boxes.shape[1]
    half_edge = box_edge // 2
    tile_extent = 2 * box_edge
    devices = lax.axis_size("dev")
    position = lax.axis_index("dev")
    squares = grain_boxes * grain_boxes
    offsets = (box_anchors[:, 0] - position + 1) % devices - 1
    tile_terms = jnp.zeros((4, half_edge, tile_extent, tile_extent), jnp.float32)
    for slot_index in range(box_count):
        placed = place_square(squares[slot_index], box_anchors[slot_index], half_edge)
        for half_index in range(2):
            target = offsets[slot_index] + half_index + 1
            current = lax.dynamic_index_in_dim(tile_terms, target, 0, keepdims=False)
            piece = placed[half_index * half_edge : (half_index + 1) * half_edge]
            tile_terms = lax.dynamic_update_index_in_dim(tile_terms, current + piece, target, 0)
    carried = tile_terms[3]
    for relay_level in (2, 1):
        carried = from_behind(carried, "dev", 1) + tile_terms[relay_level]
    covered = carried + from_behind(tile_terms[0], "dev", -1)
    nearby = [from_behind(covered, "dev", 1), covered]
    onward = covered
    for relay_level in range(2):
        onward = from_behind(onward, "dev", -1)
        nearby.append(onward)
    stacked = jnp.stack(nearby)
    pieces = []
    for slot_index in range(box_count):
        halves = []
        for half_index in range(2):
            target = offsets[slot_index] + half_index + 1
            tile_sum = lax.dynamic_index_in_dim(stacked, target, 0, keepdims=False)
            halves.append(extract_window(tile_sum, box_anchors[slot_index], box_edge))
        window = jnp.concatenate(halves, axis=0)
        pieces.append(window - squares[slot_index])
    others = jnp.stack(pieces)
    right_slot = migrations[0, 0]
    left_slot = migrations[0, 1]
    relaxed = relax_steps(grain_boxes, others)
    going_right = lax.dynamic_index_in_dim(relaxed, right_slot, 0, keepdims=False)
    going_left = lax.dynamic_index_in_dim(relaxed, left_slot, 0, keepdims=False)
    from_left = from_behind(going_right, "dev", 1)
    from_right = from_behind(going_left, "dev", -1)
    relaxed = lax.dynamic_update_index_in_dim(relaxed, from_left, right_slot, 0)
    relaxed = lax.dynamic_update_index_in_dim(relaxed, from_right, left_slot, 0)
    return relaxed


def solution(mesh):
    in_specs = (P("dev", None, None), P("dev", None), P("dev", None))
    out_specs = P("dev", None, None)
    return jax.shard_map(
        on_device, mesh=mesh, in_specs=in_specs, out_specs=out_specs, check_vma=False
    )
```

profile of v0, /device:TPU:0, one launch (start us, length us, event | category | flops | bytes accessed | tf_op | source)
XLA Modules:
  0.0 248.9 jit_solution(11776844424137229057)
XLA Ops:
  10.8 2.5 mul.127
  15.7 2.0 dot_general.22
  19.5 3.4 %fusion.1 = f32[64,128,128]{2,1,0:T(8,128)} fusion(s32[]{:T(128)S(6)} %select_n.159, f32[64,128,128]{2,1,0:T(8,128)S(1)} %pad.31), kind=kLoop, calls=%fused_computation.6 | loop fusion | flops 1048576 | bytes 8388612 | tf_op jit(solution)/shard_map/jit(_roll_dynamic)/concatenate | solution.py:73
  22.9 4.3 %broadcast_in_dim.77 = f32[4,32,128,128]{3,2,1,0:T(8,128)} broadcast(f32[]{:T(128)} %constant.172.clone.1), dimensions={} | broadcast | bytes 8388612 | tf_op jit(solution)/shard_map/broadcast_in_dim | solution.py:99
  28.7 1.7 constant_dynamic-slice_fusion.2
  30.5 1.6 fusion.26
  34.1 2.5 %pad.32 = f32[64,128,128]{2,1,0:T(8,128)} pad(f32[64,64,128]{2,1,0:T(8,128)S(1)} %fusion.40, f32[]{:T(128)} %constant.172.clone.1), padding=0_0x0_64x0_0 | pad | bytes 6291460 | tf_op jit(solution)/shard_map/jit(_pad)/pad | solution.py:72
  36.7 1.7 constant_dynamic-slice_fusion.1
  38.4 3.5 %fusion = f32[64,128,128]{2,1,0:T(8,128)S(1)} fusion(s32[]{:T(128)S(6)} %select_n.161, f32[64,128,128]{2,1,0:T(8,128)} %pad.32), kind=kLoop, calls=%fused_computation.5 | loop fusion | flops 1048576 | bytes 8388612 | tf_op jit(solution)/shard_map/jit(_roll_dynamic)/concatenate | solution.py:73
  42.0 1.9 fusion.24
  44.6 1.9 constant_dynamic-slice_fusion
  49.0 2.5 %slice_bitcast_fusion.3 = (f32[32,128,128]{2,1,0:T(8,128)S(1)}, f32[32,128,128]{2,1,0:T(8,128)S(1)}) fusion(f32[4,32,128,128]{3,2,1,0:T(8,128)} %fusion.22), kind=kLoop, calls=%fused_computation.41 | loop fusion | bytes 8388608 | tf_op jit(solution)/shard_map/squeeze | solution.py:107
  51.6 8.5 %collective-permute-start.2 = (f32[32,128,128]{2,1,0:T(8,128)S(1)}, f32[32,128,128]{2,1,0:T(8,128)S(1)}, u32[]{:S(2)}, u32[]{:S(2)}) collective-permute-start(f32[32,128,128]{2,1,0:T(8,128)S(1)} %get-tuple-element.12), channel_id=1, source_target_pairs={{0,127},{1,0},{2,1},{3,2},{4,3},{5,4},{6,5},{7,6},{8,7},{9,8},{10,... | collective-permute-start | bytes 6291464 | tf_op jit(solution)/shard_map/ppermute | solution.py:19
  60.1 23.6 %collective-permute-done = f32[32,128,128]{2,1,0:T(8,128)S(1)} collective-permute-done((f32[32,128,128]{2,1,0:T(8,128)S(1)}, f32[32,128,128]{2,1,0:T(8,128)S(1)}, u32[]{:S(2)}, u32[]{:S(2)}) %collective-permute-start) | collective-permute-done | bytes 2097184 | tf_op jit(solution)/shard_map/ppermute | solution.py:19
  83.7 1.9 fusion.20
  85.9 30.9 %collective-permute-done.1 = f32[32,128,128]{2,1,0:T(8,128)S(1)} collective-permute-done((f32[32,128,128]{2,1,0:T(8,128)S(1)}, f32[32,128,128]{2,1,0:T(8,128)S(1)}, u32[]{:S(2)}, u32[]{:S(2)}) %collective-permute-start.1) | collective-permute-done | bytes 2097184 | tf_op jit(solution)/shard_map/ppermute | solution.py:19
  116.8 3.6 %fusion.19 = f32[32,128,128]{2,1,0:T(8,128)} fusion(f32[32,128,128]{2,1,0:T(8,128)S(1)} %collective-permute-done.2, f32[32,128,128]{2,1,0:T(8,128)S(1)} %collective-permute-done.1, f32[4,32,128,128]{3,2,1,0:T(8,128)} %fusion.22), kind=kLoop, calls=%fused_computation.38 | loop fusion | flops 1048576 | bytes 8388608 | tf_op jit(solution)/shard_map/add | solution.py:110
  124.3 2.4 fusion.79
  127.2 17.1 %collective-permute-done.4 = f32[32,128,128]{2,1,0:T(8,128)} collective-permute-done((f32[32,128,128]{2,1,0:T(8,128)}, f32[32,128,128]{2,1,0:T(8,128)}, u32[]{:S(2)}, u32[]{:S(2)}) %collective-permute-start.4) | collective-permute-done | bytes 2097184 | tf_op jit(solution)/shard_map/ppermute | solution.py:19
  144.3 7.3 %collective-permute-start.5 = (f32[32,128,128]{2,1,0:T(8,128)}, f32[32,128,128]{2,1,0:T(8,128)S(1)}, u32[]{:S(2)}, u32[]{:S(2)}) collective-permute-start(f32[32,128,128]{2,1,0:T(8,128)} %collective-permute-done.4), channel_id=1, source_target_pairs={{0,127},{1,0},{2,1},{3,2},{4,3},{5,4},{6,5},{7,6},{8,7},{9,8},{10,... | collective-permute-start | bytes 6291464 | tf_op jit(solution)/shard_map/ppermute | solution.py:19
  151.6 2.8 %fusion.80 = (f32[2,64,4032]{2,1,0:T(8,128)}, f32[2,64,4032]{2,1,0:T(8,128)}) fusion(f32[2,64,4096]{2,1,0:T(8,128)S(1)} %copy-done), kind=kLoop, calls=%fused_computation.133 | loop fusion | bytes 8257536 | tf_op jit(solution)/shard_map/slice | solution.py:29
  154.4 2.8 %fusion.81 = (f32[2,64,4095]{2,1,0:T(8,128)}, f32[2,64,4095]{2,1,0:T(8,128)}) fusion(f32[2,64,4096]{2,1,0:T(8,128)S(1)} %copy-done), kind=kLoop, calls=%fused_computation.134 | loop fusion | bytes 8386560 | tf_op jit(solution)/shard_map/slice | solution.py:34
  157.8 17.7 %collective-permute-done.5 = f32[32,128,128]{2,1,0:T(8,128)S(1)} collective-permute-done((f32[32,128,128]{2,1,0:T(8,128)}, f32[32,128,128]{2,1,0:T(8,128)S(1)}, u32[]{:S(2)}, u32[]{:S(2)}) %collective-permute-start.5) | collective-permute-done | bytes 2097184 | tf_op jit(solution)/shard_map/ppermute | solution.py:19
  175.5 2.6 %pad_maximum_fusion = f32[4,32,128,128]{3,2,1,0:T(8,128)S(1)} fusion(f32[1,32,128,128]{3,2,1,0:T(8,128)S(1)} %bitcast.93, f32[1,32,128,128]{3,2,1,0:T(8,128)} %bitcast.27, f32[1,32,128,128]{3,2,1,0:T(8,128)} %bitcast.26, f32[1,32,128,128]{3,2,1,0:T(8,128)S(1)} %bitcast.92), kind=kLoop, calls=%fused_computation.4 | loop fusion | flops 6291456 | bytes 16777216 | tf_op jit(solution)/shard_map/stack | solution.py:116
  178.1 2.8 %dynamic-slice_bitcast_fusion.3 = (f32[32,128,128]{2,1,0:T(8,128)S(1)}, f32[32,128,128]{2,1,0:T(8,128)}, f32[32,128,128]{2,1,0:T(8,128)}, f32[32,128,128]{2,1,0:T(8,128)}) fusion(f32[4,32,128,128]{3,2,1,0:T(8,128)S(1)} %pad_maximum_fusion, s32[]{:T(128)S(6)} %select_n.134, s32[]{:T(128)S(6)} %select_n.138, s32[]{:T(128)S(6)} %select_n.136, s32[]{:T(128)S(6)} %select_n.135), kind=kLoop, calls=%fused_computation.57 | loop fusion | bytes 16777232 | tf_op jit(solution)/shard_map/jit(dynamic_index_in_dim)/squeeze | solution.py:122
  193.2 2.5 %maximum_subtract_fusion = (f32[1,64,4096]{2,1,0:T(8,128)S(1)}, f32[1,64,4096]{2,1,0:T(8,128)S(1)}) fusion(f32[1,32,4096]{2,1,0:T(8,128)} %concatenate.95, f32[1,32,4096]{2,1,0:T(8,128)} %concatenate.94, f32[2,64,4096]{2,1,0:T(8,128)} %copy-done.1, f32[1,32,4096]{2,1,0:T(8,128)} %concatenate.98, f32[1,32,4096]{2,1,0:T(8,128)} %concatenate.97), kind=kLoop, calls=%fused_computation.62 | loop fusion | flops 1048576 | bytes 6291456 | tf_op jit(solution)/shard_map/sub | solution.py:125
  197.3 4.2 %fusion.5 = f32[2,64,4096]{2,1,0:T(8,128)S(1)} fusion(f32[2,64,4096]{2,1,0:T(8,128)S(1)} %copy-done, f32[2,64,4095]{2,1,0:T(8,128)} %get-tuple-element.42, f32[2,64,4095]{2,1,0:T(8,128)} %get-tuple-element.41, f32[2,64,4032]{2,1,0:T(8,128)} %get-tuple-element.40, f32[2,64,4032]{2,1,0:T(8,128)S(1)} %copy-done.8, f32[2,63,4096]{2,1,0:T(8,128)S(1)} %copy-done.7, ...), kind=kLoop, calls=%fused_computation.22 | loop fusion | flops 10485760 | bytes 18750464 | tf_op jit(solution)/shard_map/add | solution.py:51
  203.3 2.5 %fusion.9 = f32[2,64,4096]{2,1,0:T(8,128)S(1)} fusion(f32[2,64,4096]{2,1,0:T(8,128)S(1)} %fusion.5, f32[2,64,4095]{2,1,0:T(8,128)S(1)} %get-tuple-element.32, f32[2,64,4095]{2,1,0:T(8,128)S(1)} %get-tuple-element.31, f32[2,64,4032]{2,1,0:T(8,128)S(1)} %get-tuple-element.30, f32[2,64,4032]{2,1,0:T(8,128)S(1)} %get-tuple-element.29, ...), kind=kLoop, calls=%fused_computation.26 | loop fusion | flops 10485760 | bytes 18750464 | tf_op jit(solution)/shard_map/add | solution.py:51
  207.7 2.3 fusion.13
  211.9 2.3 fusion.17
  217.2 18.0 %collective-permute-done.6 = f32[64,4096]{1,0:T(8,128)S(1)} collective-permute-done((f32[64,4096]{1,0:T(8,128)}, f32[64,4096]{1,0:T(8,128)S(1)}, u32[]{:S(2)}, u32[]{:S(2)}) %collective-permute-start.6) | collective-permute-done | bytes 1048608 | tf_op jit(solution)/shard_map/ppermute | solution.py:19
  235.5 12.3 %collective-permute-done.7 = f32[64,4096]{1,0:T(8,128)S(1)} collective-permute-done((f32[64,4096]{1,0:T(8,128)S(1)}, f32[64,4096]{1,0:T(8,128)S(1)}, u32[]{:S(2)}, u32[]{:S(2)}) %collective-permute-start.7) | collective-permute-done | bytes 1048608 | tf_op jit(solution)/shard_map/ppermute | solution.py:19
  (68 shorter events, 37.6 us)
Async XLA Ops:
  13.3 1.3 copy-start.1
  22.9 4.3 %copy-start.4 = (f32[64,128,128]{2,1,0:T(8,128)S(1)}, f32[64,128,128]{2,1,0:T(8,128)}, u32[]{:S(2)}) copy-start(f32[64,128,128]{2,1,0:T(8,128)} %fusion.1) | copy-start | bytes 12582916
  41.9 2.7 %copy-start.2 = (f32[64,128,128]{2,1,0:T(8,128)}, f32[64,128,128]{2,1,0:T(8,128)S(1)}, u32[]{:S(2)}) copy-start(f32[64,128,128]{2,1,0:T(8,128)S(1)} %fusion) | copy-start | bytes 12582916
  44.6 2.8 %copy-start.3 = (f32[64,128,128]{2,1,0:T(8,128)S(1)}, f32[64,128,128]{2,1,0:T(8,128)}, u32[]{:S(2)}) copy-start(f32[64,128,128]{2,1,0:T(8,128)} %copy-done.2) | copy-start | bytes 12582916
  51.5 32.2 %collective-permute-start = (f32[32,128,128]{2,1,0:T(8,128)S(1)}, f32[32,128,128]{2,1,0:T(8,128)S(1)}, u32[]{:S(2)}, u32[]{:S(2)}) collective-permute-start(f32[32,128,128]{2,1,0:T(8,128)S(1)} %get-tuple-element.11), channel_id=1, source_target_pairs={{0,1},{1,2},{2,3},{3,4},{4,5},{5,6},{6,7},{7,8},{8,9},{9,10},{10,1... | collective-permute-start | bytes 6291464 | tf_op jit(solution)/shard_map/ppermute | solution.py:19
  51.6 34.3 %collective-permute-start.2 = (f32[32,128,128]{2,1,0:T(8,128)S(1)}, f32[32,128,128]{2,1,0:T(8,128)S(1)}, u32[]{:S(2)}, u32[]{:S(2)}) collective-permute-start(f32[32,128,128]{2,1,0:T(8,128)S(1)} %get-tuple-element.12), channel_id=1, source_target_pairs={{0,127},{1,0},{2,1},{3,2},{4,3},{5,4},{6,5},{7,6},{8,7},{9,8},{10,... | collective-permute-start | bytes 6291464 | tf_op jit(solution)/shard_map/ppermute | solution.py:19
  85.6 36.1 %copy-start.9 = (s32[1,2]{1,0:T(1,128)S(1)}, s32[1,2]{1,0:T(1,128)}, u32[]{:S(2)}) copy-start(s32[1,2]{1,0:T(1,128)} %param.9) | copy-start | bytes 28
  85.6 31.1 %collective-permute-start.1 = (f32[32,128,128]{2,1,0:T(8,128)S(1)}, f32[32,128,128]{2,1,0:T(8,128)S(1)}, u32[]{:S(2)}, u32[]{:S(2)}) collective-permute-start(f32[32,128,128]{2,1,0:T(8,128)S(1)} %fusion.20), channel_id=1, source_target_pairs={{0,1},{1,2},{2,3},{3,4},{4,5},{5,6},{6,7},{7,8},{8,9},{9,10},{10,1... | collective-permute-start | bytes 6291464 | tf_op jit(solution)/shard_map/ppermute | solution.py:19
  116.8 7.5 %copy-start = (f32[2,64,4096]{2,1,0:T(8,128)S(1)}, f32[2,64,4096]{2,1,0:T(8,128)}, u32[]{:S(2)}) copy-start(f32[2,64,4096]{2,1,0:T(8,128)} %param.7) | copy-start | bytes 6291460
  120.4 23.9 %collective-permute-start.4 = (f32[32,128,128]{2,1,0:T(8,128)}, f32[32,128,128]{2,1,0:T(8,128)}, u32[]{:S(2)}, u32[]{:S(2)}) collective-permute-start(f32[32,128,128]{2,1,0:T(8,128)} %fusion.19), channel_id=1, source_target_pairs={{0,127},{1,0},{2,1},{3,2},{4,3},{5,4},{6,5},{7,6},{8,7},{9,8},{10,... | collective-permute-start | bytes 6291464 | tf_op jit(solution)/shard_map/ppermute | solution.py:19
  126.7 31.1 %collective-permute-start.3 = (f32[32,128,128]{2,1,0:T(8,128)}, f32[32,128,128]{2,1,0:T(8,128)S(1)}, u32[]{:S(2)}, u32[]{:S(2)}) collective-permute-start(f32[32,128,128]{2,1,0:T(8,128)} %fusion.19), channel_id=1, source_target_pairs={{0,1},{1,2},{2,3},{3,4},{4,5},{5,6},{6,7},{7,8},{8,9},{9,10},{10,1... | collective-permute-start | bytes 6291464 | tf_op jit(solution)/shard_map/ppermute | solution.py:19
  144.3 31.2 %collective-permute-start.5 = (f32[32,128,128]{2,1,0:T(8,128)}, f32[32,128,128]{2,1,0:T(8,128)S(1)}, u32[]{:S(2)}, u32[]{:S(2)}) collective-permute-start(f32[32,128,128]{2,1,0:T(8,128)} %collective-permute-done.4), channel_id=1, source_target_pairs={{0,127},{1,0},{2,1},{3,2},{4,3},{5,4},{6,5},{7,6},{8,7},{9,8},{10,... | collective-permute-start | bytes 6291464 | tf_op jit(solution)/shard_map/ppermute | solution.py:19
  193.2 2.9 %copy-start.6 = (f32[2,63,4096]{2,1,0:T(8,128)S(1)}, f32[2,63,4096]{2,1,0:T(8,128)}, u32[]{:S(2)}) copy-start(f32[2,63,4096]{2,1,0:T(8,128)} %get-tuple-element.37) | copy-start | bytes 6193156
  193.2 3.5 %copy-start.7 = (f32[2,63,4096]{2,1,0:T(8,128)S(1)}, f32[2,63,4096]{2,1,0:T(8,128)}, u32[]{:S(2)}) copy-start(f32[2,63,4096]{2,1,0:T(8,128)} %get-tuple-element.38) | copy-start | bytes 6193156
  193.2 4.1 %copy-start.8 = (f32[2,64,4032]{2,1,0:T(8,128)S(1)}, f32[2,64,4032]{2,1,0:T(8,128)}, u32[]{:S(2)}) copy-start(f32[2,64,4032]{2,1,0:T(8,128)} %get-tuple-element.39) | copy-start | bytes 6193156
  215.3 19.9 %collective-permute-start.6 = (f32[64,4096]{1,0:T(8,128)}, f32[64,4096]{1,0:T(8,128)S(1)}, u32[]{:S(2)}, u32[]{:S(2)}) collective-permute-start(f32[64,4096]{1,0:T(8,128)} %dynamic-slice_bitcast_fusion.5), channel_id=1, source_target_pairs={{0,1},{1,2},{2,3},{3,4},{4,5},{5,6},{6,7},{7,8},{8,9},{9,10},{10,1... | collective-permute-start | bytes 3145736 | tf_op jit(solution)/shard_map/ppermute | solution.py:19
  235.4 12.4 %copy-start.5 = (f32[2,64,4096]{2,1,0:T(8,128)}, f32[2,64,4096]{2,1,0:T(8,128)S(1)}, u32[]{:S(2)}) copy-start(f32[2,64,4096]{2,1,0:T(8,128)S(1)} %get-tuple-element.14) | copy-start | bytes 6291460
  235.4 12.4 %collective-permute-start.7 = (f32[64,4096]{1,0:T(8,128)S(1)}, f32[64,4096]{1,0:T(8,128)S(1)}, u32[]{:S(2)}, u32[]{:S(2)}) collective-permute-start(f32[64,4096]{1,0:T(8,128)S(1)} %get-tuple-element.13), channel_id=1, source_target_pairs={{0,127},{1,0},{2,1},{3,2},{4,3},{5,4},{6,5},{7,6},{8,7},{9,8},{10,... | collective-permute-start | bytes 3145736 | tf_op jit(solution)/shard_map/ppermute | solution.py:19
where the time goes:
time: 249 us
  waiting for transfers between devices  120 us (48%)
  local copies, waits for them, and re-layouts  51.2 us (21%)
  other arithmetic  42.3 us (17%)
  starting transfers between devices  16.7 us (7%)
  between operations  13.5 us (5%)
  matrix products  5.01 us (2%)
    ppermute x8, waiting for transfers between devices, from_behind(): return lax.ppermute(value, axis, pairs)  120 us
    ppermute x8, starting transfers between devices, from_behind(): return lax.ppermute(value, axis, pairs)  16.7 us
    add x4, other arithmetic, relax_steps(): order_field = order_field + time_step * driving  11.3 us
    concatenate x2, other arithmetic, place_square(): return jnp.roll(spread, anchor[1] * half_edge, axis=1)  6.95 us
    dynamic_slice x3, local copies, waits for them, and re-layouts, on_device(): current = lax.dynamic_index_in_dim(tile_terms, target, 0, keepdims=False)  5.34 us
    dynamic_update_slice x3, other arithmetic, on_device(): lax.dynamic_update_index_in_dim(tile_terms, current + piece, target, 0)  5.12 us
  transfers between devices with their start and end apart: 8, of which 7 were waited for; matrix products, arithmetic and copies ran while one was open for 4% of the time, Pallas kernels for 0%

commit v1 on v0

v1 whole, which is shorter than its diff:
```python
import functools

import jax
import jax.numpy as jnp
from jax import lax
from jax.experimental import pallas as pl
from jax.experimental.pallas import tpu as pltpu
from jax.sharding import PartitionSpec as P

SUBSTEPS = 4

growth_rate = 1.0
quartic_rate = 1.0
coupling = 1.5
gradient_energy = 2.0
time_step = 0.02

HALF_BLOCKS = 128
PIECE = (HALF_BLOCKS, 8, 128)
TILE = (2, 64, 4, 8, 128)


def meta_int(ref, index):
    return ref[0, 0, index].astype(jnp.int32)


def box_meta(ref, slot, flip):
    offset = jnp.where(slot == 0, meta_int(ref, 0), meta_int(ref, 1))
    row = jnp.where(slot == 0, meta_int(ref, 2), meta_int(ref, 3)) & 3
    column = jnp.where(slot == 0, meta_int(ref, 4), meta_int(ref, 5)) & 3
    return jnp.where(flip == 1, -offset, offset), row, column


def deposit(tile_ref, piece_ref, base, row, column):
    lane = lax.broadcasted_iota(jnp.int32, (8, 128), 1)
    inside = ((lane - 32 * column) & 127) < 64
    shift = 32 * column
    shift_odd = (32 * column + 64) & 127

    def body(step, carry):
        for sub in range(2):
            m = step * 2 + sub
            place = (16 * row + m) & 63
            for it in range(4):
                value = piece_ref[base + it * 32 + m]
                value = value * value
                even = jnp.where(inside, pltpu.roll(value, shift, 1), 0.0)
                odd = jnp.where(inside, pltpu.roll(value, shift_odd, 1), 0.0)
                tile_ref[0, place, it] += even
                tile_ref[1, place, it] += odd
        return carry

    lax.fori_loop(0, 16, body, 0)


def extract(tile_ref, out_ref, row, column):
    lane = lax.broadcasted_iota(jnp.int32, (8, 128), 1)
    low = lane < 64
    shift = (128 - 32 * column) & 127
    shift_odd = (64 - 32 * column) & 127

    def body(step, carry):
        for sub in range(2):
            m = step * 2 + sub
            place = (16 * row + m) & 63
            for it in range(4):
                even = pltpu.roll(tile_ref[0, place, it], shift, 1)
                odd = pltpu.roll(tile_ref[1, place, it], shift_odd, 1)
                out_ref[it * 32 + m] = jnp.where(low, even, odd)
        return carry

    lax.fori_loop(0, 16, body, 0)


def deposit_if(cond, tile_ref, piece_ref, slot, row, column):
    @pl.when(cond)
    def _():
        deposit(tile_ref, piece_ref, slot * HALF_BLOCKS, row, column)


def clear(tile_ref):
    def body(place, carry):
        for par in range(2):
            for it in range(4):
                tile_ref[par, place, it] = jnp.zeros((8, 128), jnp.float32)
        return carry

    lax.fori_loop(0, 64, body, 0)


def local_kernel(mine_outer, mine_inner, sib_outer, sib_inner, mine_meta, sib_meta, tile_0, tile_1):
    flip = meta_int(mine_meta, 8)
    clear(tile_0)
    clear(tile_1)
    for slot in range(2):
        u, row, column = box_meta(mine_meta, slot, flip)
        deposit_if(u == 0, tile_0, mine_outer, slot, row, column)
        deposit_if(u == -1, tile_0, mine_inner, slot, row, column)
        deposit_if(u == 1, tile_1, mine_outer, slot, row, column)
        deposit_if(u == 0, tile_1, mine_inner, slot, row, column)
        u, row, column = box_meta(sib_meta, slot, flip)
        deposit_if(u == -1, tile_0, sib_inner, slot, row, column)
        deposit_if(u == 0, tile_1, sib_inner, slot, row, column)
        deposit_if(u == -1, tile_1, sib_outer, slot, row, column)


def heading_outer(ref, flip):
    return jnp.where(flip == 1, meta_int(ref, 7), meta_int(ref, 6)) & 1


def inner_kernel(part, out_outer, beyond, mine_meta, sib_meta, out_meta, beyond_meta,
                 to_next, to_next_far, window_out, window_sib, tile, sem):
    copy = pltpu.make_async_copy(part, tile, sem)
    copy.start()
    copy.wait()
    flip = meta_int(mine_meta, 8)
    for slot in range(2):
        u, row, column = box_meta(out_meta, slot, flip)
        deposit_if(u == 1, tile, out_outer, slot, row, column)
        u, row, column = box_meta(beyond_meta, slot, flip)
        deposit_if(u == -1, tile, beyond, slot, row, column)
    leaving = heading_outer(sib_meta, flip)
    _, row, column = box_meta(sib_meta, leaving, flip)
    extract(tile, to_next, row, column)
    _, row, column = box_meta(beyond_meta, heading_outer(beyond_meta, flip), flip)
    extract(tile, to_next_far, row, column)
    _, row, column = box_meta(out_meta, heading_outer(out_meta, flip), flip)
    extract(tile, window_out, row, column)
    _, row, column = box_meta(sib_meta, 1 - leaving, flip)
    extract(tile, window_sib, row, column)


def outer_kernel(part, out_outer, out_inner, far_inner, mine_meta, sib_meta, out_meta, far_meta,
                 to_next, to_sib, window_out, window_sib, tile, sem):
    copy = pltpu.make_async_copy(part, tile, sem)
    copy.start()
    copy.wait()
    flip = meta_int(mine_meta, 8)
    for slot in range(2):
        u, row, column = box_meta(out_meta, slot, flip)
        deposit_if(u == 0, tile, out_outer, slot, row, column)
        deposit_if(u == 1, tile, out_inner, slot, row, column)
        u, row, column = box_meta(far_meta, slot, flip)
        deposit_if(u == 1, tile, far_inner, slot, row, column)
    leaving = heading_outer(sib_meta, flip)
    _, row, column = box_meta(sib_meta, leaving, flip)
    extract(tile, to_next, row, column)
    _, row, column = box_meta(mine_meta, heading_outer(mine_meta, flip), flip)
    extract(tile, to_sib, row, column)
    _, row, column = box_meta(out_meta, heading_outer(out_meta, flip), flip)
    extract(tile, window_out, row, column)
    _, row, column = box_meta(sib_meta, 1 - leaving, flip)
    extract(tile, window_sib, row, column)


def substep(source, target, factor):
    shape = (8, 128)
    lane = lax.broadcasted_iota(jnp.int32, shape, 1)
    sublane = lax.broadcasted_iota(jnp.int32, shape, 0)
    low = lane < 64
    last_z = (lane & 63) == 63
    first_z = (lane & 63) == 0
    top = sublane == 7
    bottom = sublane == 0
    zero = jnp.zeros(shape, jnp.float32)

    def swapped(m):
        return [pltpu.roll(source[it * 32 + m], 64, 1) for it in range(8)]

    def body(m, carry):
        before, here = carry
        following = jnp.minimum(m + 1, 31)
        after = [jnp.where(m == 31, zero, value) for value in swapped(following)]
        cells = [source[it * 32 + m] for it in range(8)]
        ups = [pltpu.roll(value, 7, 0) for value in cells] + [zero]
        downs = [zero] + [pltpu.roll(value, 1, 0) for value in cells]
        for it in range(8):
            value = cells[it]
            beside = jnp.where(top, ups[it + 1], ups[it])
            beside += jnp.where(bottom, downs[it], downs[it + 1])
            beside += here[it] + jnp.where(low, before[it], after[it])
            beside += jnp.where(last_z, 0.0, pltpu.roll(value, 127, 1))
            beside += jnp.where(first_z, 0.0, pltpu.roll(value, 1, 1))
            rate = factor[it * 32 + m] - (time_step * quartic_rate) * (value * value)
            target[it * 32 + m] = value * rate + (time_step * gradient_energy) * beside
        return here, after

    lax.fori_loop(0, 32, body, ([zero] * 8, swapped(0)))


def relax_kernel(scalars, *refs, first):
    (half_0, half_1), windows, rest = refs[:2], refs[2:6], refs[6:]
    result, factor, ping, pong = rest[-4:]
    flip, u = scalars[1], scalars[2]
    base = 1.0 + time_step * (growth_rate - 6.0 * gradient_energy)
    scale = 2.0 * coupling * time_step

    for g, half in ((0, half_0), (1, half_1)):
        at = pl.multiple_of(jnp.where(flip == 1, 1 - g, g) * HALF_BLOCKS, HALF_BLOCKS)
        tile = first + u + g
        for index, window in enumerate(windows):
            @pl.when(tile == first - 1 + index)
            def _(window=window, half=half, at=at):
                def body(n, carry):
                    for sub in range(8):
                        value = half[n * 8 + sub]
                        ping[at + n * 8 + sub] = value
                        factor[at + n * 8 + sub] = base - scale * (window[n * 8 + sub] - value * value)
                    return carry

                lax.fori_loop(0, HALF_BLOCKS // 8, body, 0)

    substep(ping, pong, factor)
    substep(pong, ping, factor)
    substep(ping, pong, factor)
    substep(pong, result.at[0], factor)


def whole(shape):
    return pl.BlockSpec(shape, lambda *_: (0,) * len(shape))


def piece_of_message():
    return pl.BlockSpec((2 * HALF_BLOCKS, 8, 128), lambda *_: (0, 0, 0))


def meta_of_message():
    return pl.BlockSpec((1, 8, 128), lambda *_: (2 * HALF_BLOCKS, 0, 0), memory_space=pltpu.SMEM)


def on_device(grain_boxes, box_anchors, migrations):
    devices = lax.axis_size("dev")
    position = lax.axis_index("dev")
    parity = position % 2
    chips = devices // 2

    def pairs_of(even_step, odd_step):
        pairs = []
        for chip in range(chips):
            pairs.append((2 * chip, (2 * chip + even_step) % devices))
            pairs.append((2 * chip + 1, (2 * chip + 1 + odd_step) % devices))
        return pairs

    sibling, outward = pairs_of(1, -1), pairs_of(-1, 1)
    inward, inward_far = pairs_of(2, -2), pairs_of(3, -3)

    def send(value, pairs):
        return lax.ppermute(value, "dev", pairs)

    boxes = grain_boxes.reshape(2, 8, 8, 32, 128).transpose(0, 1, 3, 2, 4)
    offsets = (box_anchors[:, 0] - position + 1) % devices - 1
    meta = jnp.concatenate(
        [offsets, box_anchors[:, 1], box_anchors[:, 2], migrations[0], parity[None]]
    ).astype(jnp.float32)
    meta = jnp.pad(meta.reshape(1, 1, 9), ((0, 0), (0, 7), (0, 119)))

    def message(start):
        part = lax.dynamic_slice_in_dim(boxes, start, 4, 1)
        return jnp.concatenate([part.reshape(2 * HALF_BLOCKS, 8, 128), meta])

    outer = message(parity * 4)
    inner = message(4 - parity * 4)

    out_outer = send(outer, outward)
    out_inner = send(inner, outward)
    far_inner = send(inner, inward)
    sib_outer = send(outer, sibling)
    sib_inner = send(inner, sibling)
    beyond = send(out_outer, sibling)

    data, info = piece_of_message(), meta_of_message()
    tile_type = jax.ShapeDtypeStruct(TILE, jnp.float32)
    piece_type = jax.ShapeDtypeStruct(PIECE, jnp.float32)
    params = pltpu.CompilerParams(vmem_limit_bytes=48 << 20)
    part_0, part_1 = pl.pallas_call(
        local_kernel,
        grid=(1,),
        in_specs=[data] * 4 + [info] * 2,
        out_specs=[whole(TILE)] * 2,
        out_shape=[tile_type] * 2,
        compiler_params=params,
        name="local_tiles",
    )(outer, inner, sib_outer, sib_inner, outer, sib_outer)

    hbm = pl.BlockSpec(memory_space=pl.ANY)
    scratch = [pltpu.VMEM(TILE, jnp.float32), pltpu.SemaphoreType.DMA(())]
    to_next, to_next_far, window_out_1, window_sib_1 = pl.pallas_call(
        inner_kernel,
        grid=(1,),
        in_specs=[hbm] + [data] * 2 + [info] * 4,
        out_specs=[whole(PIECE)] * 4,
        out_shape=[piece_type] * 4,
        scratch_shapes=scratch,
        compiler_params=params,
        name="inner_tile",
    )(part_1, out_outer, beyond, outer, sib_outer, out_outer, beyond)
    near_out = send(to_next, inward)
    near_sib = send(to_next_far, inward_far)

    to_next, to_sib, window_out_0, window_sib_0 = pl.pallas_call(
        outer_kernel,
        grid=(1,),
        in_specs=[hbm] + [data] * 3 + [info] * 4,
        out_specs=[whole(PIECE)] * 4,
        out_shape=[piece_type] * 4,
        scratch_shapes=scratch,
        compiler_params=params,
        name="outer_tile",
    )(part_0, out_outer, out_inner, far_inner, outer, sib_outer, out_outer, far_inner)
    far_out = send(to_next, inward)
    from_sib = send(to_sib, sibling)

    def numbers(message_meta, sign_slot, own_slot):
        values = message_meta[0, 0, :9].astype(jnp.int32)
        slot = values[sign_slot]
        offset = values[slot]
        return jnp.stack([slot, parity, jnp.where(parity == 1, -offset, offset), own_slot])

    box_type = jax.ShapeDtypeStruct((2, 2 * HALF_BLOCKS, 8, 128), jnp.float32)
    half = pl.BlockSpec(PIECE, lambda _, s: (s[0], 0, 0))
    box_out = pl.BlockSpec((1, 2 * HALF_BLOCKS, 8, 128), lambda _, s: (s[3], 0, 0, 0))
    box_scratch = [pltpu.VMEM((2 * HALF_BLOCKS, 8, 128), jnp.float32)] * 3

    def relax(name, first, scalars, halves, windows, held):
        return pl.pallas_call(
            functools.partial(relax_kernel, first=first),
            grid_spec=pltpu.PrefetchScalarGridSpec(
                num_scalar_prefetch=1,
                grid=(1,),
                in_specs=[half] * 2 + [whole(PIECE)] * 4 + [hbm] * len(held),
                out_specs=box_out,
                scratch_shapes=box_scratch,
            ),
            out_shape=box_type,
            input_output_aliases={7: 0} if held else {},
            compiler_params=params,
            name=name,
        )(scalars, *halves, *windows, *held)

    sib_scalars = numbers(sib_outer[2 * HALF_BLOCKS:], 7 - parity, migrations[0, 1 - parity])
    out_scalars = numbers(out_outer[2 * HALF_BLOCKS:], 6 + parity, migrations[0, parity])
    held = relax(
        "relax_sibling", 1, sib_scalars, (sib_inner, sib_outer),
        (window_sib_0, window_sib_1, from_sib, near_sib), (),
    )
    relaxed = relax(
        "relax_outer", -1, out_scalars, (out_inner, out_outer),
        (far_out, near_out, window_out_0, window_out_1), (held,),
    )
    return relaxed.reshape(2, 8, 32, 8, 128).transpose(0, 1, 3, 2, 4).reshape(2, 64, 4096)


def solution(mesh):
    in_specs = (P("dev", None, None), P("dev", None), P("dev", None))
    out_specs = P("dev", None, None)
    return jax.shard_map(
        on_device, mesh=mesh, in_specs=in_specs, out_specs=out_specs, check_vma=False
    )
```

time: 249 us -> 134 us (0.54)
  the two profiles are of different devices: /device:TPU:0 before, /device:TPU:1 now
where the time goes in v1:
time: 134 us; the launch traced here: 133 us
  Pallas kernels  71.1 us (53%)
  starting transfers between devices  35.1 us (26%)
  local copies, waits for them, and re-layouts  10.2 us (8%)
  between operations  6.83 us (5%)
  waiting for transfers between devices  5.01 us (4%)
  other arithmetic  5 us (4%)
    ppermute x10, starting transfers between devices, send(): return lax.ppermute(value, 'dev', pairs)  35.1 us
    pallas_call x2, Pallas kernels, relax(): pl.pallas_call(functools.partial(relax_kernel, first=first), grid_spec=pl...  32.3 us
    pallas_call x1, Pallas kernels, on_device(): pl.pallas_call(outer_kernel, grid=(1,), in_specs=[hbm] + [data] * 3 + [in...  13.8 us
    pallas_call x1, Pallas kernels, on_device(): pl.pallas_call(inner_kernel, grid=(1,), in_specs=[hbm] + [data] * 2 + [in...  13.4 us
    pallas_call x1, Pallas kernels, on_device(): pl.pallas_call(local_kernel, grid=(1,), in_specs=[data] * 4 + [info] * 2,...  11.7 us
    ppermute x10, waiting for transfers between devices, send(): return lax.ppermute(value, 'dev', pairs)  5.01 us
    unnamed x22, local copies, waits for them, and re-layouts  4.49 us
    another operation x2, other arithmetic, numbers(): jnp.stack([slot, parity, jnp.where(parity == 1, -offset, offset), own_slot])  2.78 us
  transfers between devices with their start and end apart: 10, of which 3 were waited for; matrix products, arithmetic and copies ran while one was open for 5% of the time, Pallas kernels for 41%

profile of v1, /device:TPU:1, one launch (start us, length us, event | category | flops | bytes accessed | tf_op | source)
XLA Modules:
  0.0 133.2 jit_solution(614681232006226809)
XLA Ops:
  0.0 1.0 slice_reduce_fusion
  1.0 0.8 concatenate.31
  1.8 1.7 %constant_dynamic-slice_fusion.3 = (f32[2,4,8,32,128]{4,2,3,1,0:T(8,128)S(1)}, f32[2,4,8,32,128]{4,2,3,1,0:T(8,128)S(1)}) fusion(f32[2,8,8,32,128]{4,2,3,1,0:T(8,128)} %bitcast.31, s32[]{:T(128)S(6)} %select_n.56, s32[]{:T(128)S(6)} %select_n.50), kind=kLoop, calls=%fused_computation.9 | loop fusion | bytes 4194312 | tf_op jit(solution)/shard_map/dynamic-slice.1
  3.5 0.0 copy-start.10
  3.5 1.2 fusion.1
  4.7 2.7 %collective-permute-start = (f32[257,8,128]{2,1,0:T(8,128)S(1)}, f32[257,8,128]{2,1,0:T(8,128)S(1)}, u32[]{:S(2)}, u32[]{:S(2)}) collective-permute-start(f32[257,8,128]{2,1,0:T(8,128)S(1)} %get-tuple-element.33.mine_outer.mine_meta), channel_id=1, source_target_pairs={{0,127},{1,2},{2,1},{3,4},{4,3},{5,6},{6,5},{7,8},{8,7},{9,10},{10... | collective-permute-start | bytes 3158024 | tf_op jit(solution)/shard_map/ppermute | solution.py:248
  7.4 6.9 %collective-permute-start.2 = (f32[257,8,128]{2,1,0:T(8,128)S(1)}, f32[257,8,128]{2,1,0:T(8,128)S(1)}, u32[]{:S(2)}, u32[]{:S(2)}) collective-permute-start(f32[257,8,128]{2,1,0:T(8,128)S(1)} %get-tuple-element.33.mine_outer.mine_meta), channel_id=1, source_target_pairs={{0,1},{1,0},{2,3},{3,2},{4,5},{5,4},{6,7},{7,6},{8,9},{9,8},{10,11... | collective-permute-start | bytes 3158024 | tf_op jit(solution)/shard_map/ppermute | solution.py:248
  14.3 7.3 %collective-permute-start.4 = (f32[257,8,128]{2,1,0:T(8,128)}, f32[257,8,128]{2,1,0:T(8,128)}, u32[]{:S(2)}, u32[]{:S(2)}) collective-permute-start(f32[257,8,128]{2,1,0:T(8,128)} %get-tuple-element.32.mine_inner), channel_id=1, source_target_pairs={{0,2},{1,127},{2,4},{3,1},{4,6},{5,3},{6,8},{7,5},{8,10},{9,7},{10... | collective-permute-start | bytes 3158024 | tf_op jit(solution)/shard_map/ppermute | solution.py:248
  21.6 1.4 %collective-permute-done.out_outer.out_meta.refs_1_ = f32[257,8,128]{2,1,0:T(8,128)S(1)} collective-permute-done((f32[257,8,128]{2,1,0:T(8,128)S(1)}, f32[257,8,128]{2,1,0:T(8,128)S(1)}, u32[]{:S(2)}, u32[]{:S(2)}) %collective-permute-start) | collective-permute-done | bytes 1052704 | tf_op jit(solution)/shard_map/ppermute | solution.py:248
  23.0 7.5 %collective-permute-start.6 = (f32[257,8,128]{2,1,0:T(8,128)S(1)}, f32[257,8,128]{2,1,0:T(8,128)}, u32[]{:S(2)}, u32[]{:S(2)}) collective-permute-start(f32[257,8,128]{2,1,0:T(8,128)S(1)} %collective-permute-done.out_outer.out_meta.refs_1_), channel_id=1, source_target_pairs={{0,1},{1,0},{2,3},{3,2},{4,5},{5,4},{6,7},{7,6},{8,9},{9,8},{10,11... | collective-permute-start | bytes 3158024 | tf_op jit(solution)/shard_map/ppermute | solution.py:248
  30.6 0.7 constant_dynamic-slice_fusion
  31.2 11.7 %local_tiles.1 = (f32[2,64,4,8,128]{4,3,2,1,0:T(8,128)}, f32[2,64,4,8,128]{4,3,2,1,0:T(8,128)}) custom-call(f32[257,8,128]{2,1,0:T(8,128)S(1)} %get-tuple-element.33.mine_outer.mine_meta, f32[257,8,128]{2,1,0:T(8,128)} %get-tuple-element.32.mine_inner, f32[257,8,128]{2,1,0:T(8,128)S(1)} %collective-permute-done.2.sib_outer.sib_meta.refs_1_, ...), custom_call_target="tpu_custom_call" | custom-call | tf_op jit(solution)/shard_map/local_tiles/pallas_call | solution.py:275
  42.9 2.1 %collective-permute-done.4.far_inner.far_meta = f32[257,8,128]{2,1,0:T(8,128)} collective-permute-done((f32[257,8,128]{2,1,0:T(8,128)}, f32[257,8,128]{2,1,0:T(8,128)}, u32[]{:S(2)}, u32[]{:S(2)}) %collective-permute-start.4) | collective-permute-done | bytes 1052704 | tf_op jit(solution)/shard_map/ppermute | solution.py:248
  45.0 13.8 %outer_tile.1 = (f32[128,8,128]{2,1,0:T(8,128)}, f32[128,8,128]{2,1,0:T(8,128)}, f32[128,8,128]{2,1,0:T(8,128)S(1)}, f32[128,8,128]{2,1,0:T(8,128)S(1)}) custom-call(f32[2,64,4,8,128]{4,3,2,1,0:T(8,128)} %get-tuple-element.15.part, f32[257,8,128]{2,1,0:T(8,128)S(1)} %collective-permute-done.out_outer.out_meta.refs_1_, ...), custom_call_target="tpu_custom_call" | custom-call | tf_op jit(solution)/shard_map/outer_tile/pallas_call | solution.py:300
  58.8 0.8 copy-done.4
  59.6 3.1 %collective-permute-start.8 = (f32[128,8,128]{2,1,0:T(8,128)}, f32[128,8,128]{2,1,0:T(8,128)}, u32[]{:S(2)}, u32[]{:S(2)}) collective-permute-start(f32[128,8,128]{2,1,0:T(8,128)} %get-tuple-element.23), channel_id=1, source_target_pairs={{0,1},{1,0},{2,3},{3,2},{4,5},{5,4},{6,7},{7,6},{8,9},{9,8},{10,11... | collective-permute-start | bytes 1572872 | tf_op jit(solution)/shard_map/ppermute | solution.py:248
  62.7 6.8 %collective-permute-start.5 = (f32[128,8,128]{2,1,0:T(8,128)}, f32[128,8,128]{2,1,0:T(8,128)S(1)}, u32[]{:S(2)}, u32[]{:S(2)}) collective-permute-start(f32[128,8,128]{2,1,0:T(8,128)} %get-tuple-element.16), channel_id=1, source_target_pairs={{0,2},{1,127},{2,4},{3,1},{4,6},{5,3},{6,8},{7,5},{8,10},{9,7},{10... | collective-permute-start | bytes 1572872 | tf_op jit(solution)/shard_map/ppermute | solution.py:248
  69.5 13.4 %inner_tile.1 = (f32[128,8,128]{2,1,0:T(8,128)}, f32[128,8,128]{2,1,0:T(8,128)}, f32[128,8,128]{2,1,0:T(8,128)S(1)}, f32[128,8,128]{2,1,0:T(8,128)S(1)}) custom-call(f32[2,64,4,8,128]{4,3,2,1,0:T(8,128)} %get-tuple-element.17.part, f32[257,8,128]{2,1,0:T(8,128)S(1)} %collective-permute-done.out_outer.out_meta.refs_1_, ...), custom_call_target="tpu_custom_call" | custom-call | tf_op jit(solution)/shard_map/inner_tile/pallas_call | solution.py:287
  82.9 0.8 copy-done.6
  83.7 0.8 copy-done.8
  84.5 0.8 collective-permute-start.7
  85.3 0.7 constant_dynamic-slice_fusion.2
  87.3 0.7 constant_dynamic-slice_fusion.6
  90.0 0.6 constant_dynamic-slice_fusion.1
  92.0 0.6 constant_dynamic-slice_fusion.5
  94.6 1.5 %pad_add_fusion.1.scalars = s32[4]{0:T(128)S(1)} fusion(s32[1]{0:T(128)} %bitcast.18, s32[1]{0:T(128)} %bitcast.17, s32[1]{0:T(128)} %bitcast.14, s32[1]{0:T(128)} %bitcast.7), kind=kLoop, calls=%fused_computation.24 | loop fusion | flops 12 | bytes 32 | tf_op jit(solution)/shard_map/stack | solution.py:317
  96.1 1.3 pad_add_fusion.scalars
  97.4 1.5 %collective-permute-done.9.refs_5_ = f32[128,8,128]{2,1,0:T(8,128)} collective-permute-done((f32[128,8,128]{2,1,0:T(8,128)}, f32[128,8,128]{2,1,0:T(8,128)}, u32[]{:S(2)}, u32[]{:S(2)}) %collective-permute-start.9) | collective-permute-done | bytes 524320 | tf_op jit(solution)/shard_map/ppermute | solution.py:248
  98.8 1.0 copy-done.5
  99.9 1.0 copy-done.9
  100.9 16.2 %relax_sibling.1.refs_6_ = f32[2,256,8,128]{3,2,1,0:T(8,128)} custom-call(s32[4]{0:T(128)S(1)} %pad_add_fusion.1.scalars, f32[257,8,128]{2,1,0:T(8,128)} %collective-permute-done.3.sib_inner.refs_0_, f32[257,8,128]{2,1,0:T(8,128)S(1)} %copy-done.1, f32[128,8,128]{2,1,0:T(8,128)S(1)} %copy-done.5, f32[128,8,128]{2,1,0:T(8,128)S(1)} %copy-done.9, ...), custom_call_target="tpu_custom_call" | custom-call | tf_op jit(solution)/shard_map/relax_sibling/pallas_call | solution.py:325
  117.1 16.1 %relax_outer.1 = f32[2,256,8,128]{3,2,1,0:T(8,128)} custom-call(s32[4]{0:T(128)S(1)} %pad_add_fusion.scalars, f32[257,8,128]{2,1,0:T(8,128)} %collective-permute-done.1.out_inner.refs_0_, f32[257,8,128]{2,1,0:T(8,128)S(1)} %collective-permute-done.out_outer.out_meta.refs_1_, ...), custom_call_target="tpu_custom_call", output_to_operand_aliasing={{}: (7, {})} | custom-call | tf_op jit(solution)/shard_map/relax_outer/pallas_call | solution.py:325
  (30 shorter events, 0.1 us)
Async XLA Ops:
  3.5 27.1 %copy-start.10 = (s32[1,2]{1,0:T(1,128)S(1)}, s32[1,2]{1,0:T(1,128)}, u32[]{:S(2)}) copy-start(s32[1,2]{1,0:T(1,128)} %param.5) | copy-start | bytes 28
  4.7 38.3 %copy-start.2 = (f32[257,8,128]{2,1,0:T(8,128)}, f32[257,8,128]{2,1,0:T(8,128)S(1)}, u32[]{:S(2)}) copy-start(f32[257,8,128]{2,1,0:T(8,128)S(1)} %get-tuple-element.33.mine_outer.mine_meta) | copy-start | bytes 3158020
  4.7 18.4 %collective-permute-start = (f32[257,8,128]{2,1,0:T(8,128)S(1)}, f32[257,8,128]{2,1,0:T(8,128)S(1)}, u32[]{:S(2)}, u32[]{:S(2)}) collective-permute-start(f32[257,8,128]{2,1,0:T(8,128)S(1)} %get-tuple-element.33.mine_outer.mine_meta), channel_id=1, source_target_pairs={{0,127},{1,2},{2,1},{3,4},{4,3},{5,6},{6,5},{7,8},{8,7},{9,10},{10... | collective-permute-start | bytes 3158024 | tf_op jit(solution)/shard_map/ppermute | solution.py:248
  7.4 23.9 %collective-permute-start.2 = (f32[257,8,128]{2,1,0:T(8,128)S(1)}, f32[257,8,128]{2,1,0:T(8,128)S(1)}, u32[]{:S(2)}, u32[]{:S(2)}) collective-permute-start(f32[257,8,128]{2,1,0:T(8,128)S(1)} %get-tuple-element.33.mine_outer.mine_meta), channel_id=1, source_target_pairs={{0,1},{1,0},{2,3},{3,2},{4,5},{5,4},{6,7},{7,6},{8,9},{9,8},{10,11... | collective-permute-start | bytes 3158024 | tf_op jit(solution)/shard_map/ppermute | solution.py:248
  14.3 16.9 %collective-permute-start.3 = (f32[257,8,128]{2,1,0:T(8,128)}, f32[257,8,128]{2,1,0:T(8,128)}, u32[]{:S(2)}, u32[]{:S(2)}) collective-permute-start(f32[257,8,128]{2,1,0:T(8,128)} %get-tuple-element.32.mine_inner), channel_id=1, source_target_pairs={{0,1},{1,0},{2,3},{3,2},{4,5},{5,4},{6,7},{7,6},{8,9},{9,8},{10,11... | collective-permute-start | bytes 3158024 | tf_op jit(solution)/shard_map/ppermute | solution.py:248
  14.3 28.6 %collective-permute-start.1 = (f32[257,8,128]{2,1,0:T(8,128)}, f32[257,8,128]{2,1,0:T(8,128)}, u32[]{:S(2)}, u32[]{:S(2)}) collective-permute-start(f32[257,8,128]{2,1,0:T(8,128)} %get-tuple-element.32.mine_inner), channel_id=1, source_target_pairs={{0,127},{1,2},{2,1},{3,4},{4,3},{5,6},{6,5},{7,8},{8,7},{9,10},{10... | collective-permute-start | bytes 3158024 | tf_op jit(solution)/shard_map/ppermute | solution.py:248
  14.3 30.7 %collective-permute-start.4 = (f32[257,8,128]{2,1,0:T(8,128)}, f32[257,8,128]{2,1,0:T(8,128)}, u32[]{:S(2)}, u32[]{:S(2)}) collective-permute-start(f32[257,8,128]{2,1,0:T(8,128)} %get-tuple-element.32.mine_inner), channel_id=1, source_target_pairs={{0,2},{1,127},{2,4},{3,1},{4,6},{5,3},{6,8},{7,5},{8,10},{9,7},{10... | collective-permute-start | bytes 3158024 | tf_op jit(solution)/shard_map/ppermute | solution.py:248
  23.0 46.5 %collective-permute-start.6 = (f32[257,8,128]{2,1,0:T(8,128)S(1)}, f32[257,8,128]{2,1,0:T(8,128)}, u32[]{:S(2)}, u32[]{:S(2)}) collective-permute-start(f32[257,8,128]{2,1,0:T(8,128)S(1)} %collective-permute-done.out_outer.out_meta.refs_1_), channel_id=1, source_target_pairs={{0,1},{1,0},{2,3},{3,2},{4,5},{5,4},{6,7},{7,6},{8,9},{9,8},{10,11... | collective-permute-start | bytes 3158024 | tf_op jit(solution)/shard_map/ppermute | solution.py:248
  31.2 11.7 %copy-start = (f32[257,8,128]{2,1,0:T(8,128)}, f32[257,8,128]{2,1,0:T(8,128)S(1)}, u32[]{:S(2)}) copy-start(f32[257,8,128]{2,1,0:T(8,128)S(1)} %collective-permute-done.2.sib_outer.sib_meta.refs_1_) | copy-start | bytes 3158020
  45.0 24.5 %copy-start.3 = (f32[257,8,128]{2,1,0:T(8,128)S(1)}, f32[257,8,128]{2,1,0:T(8,128)}, u32[]{:S(2)}) copy-start(f32[257,8,128]{2,1,0:T(8,128)} %copy-done.2) | copy-start | bytes 3158020
  58.8 0.8 copy-start.4
  59.6 37.8 %collective-permute-start.8 = (f32[128,8,128]{2,1,0:T(8,128)}, f32[128,8,128]{2,1,0:T(8,128)}, u32[]{:S(2)}, u32[]{:S(2)}) collective-permute-start(f32[128,8,128]{2,1,0:T(8,128)} %get-tuple-element.23), channel_id=1, source_target_pairs={{0,1},{1,0},{2,3},{3,2},{4,5},{5,4},{6,7},{7,6},{8,9},{9,8},{10,11... | collective-permute-start | bytes 1572872 | tf_op jit(solution)/shard_map/ppermute | solution.py:248
  62.7 54.4 %collective-permute-start.5 = (f32[128,8,128]{2,1,0:T(8,128)}, f32[128,8,128]{2,1,0:T(8,128)S(1)}, u32[]{:S(2)}, u32[]{:S(2)}) collective-permute-start(f32[128,8,128]{2,1,0:T(8,128)} %get-tuple-element.16), channel_id=1, source_target_pairs={{0,2},{1,127},{2,4},{3,1},{4,6},{5,3},{6,8},{7,5},{8,10},{9,7},{10... | collective-permute-start | bytes 1572872 | tf_op jit(solution)/shard_map/ppermute | solution.py:248
  69.5 15.8 %copy-start.1 = (f32[257,8,128]{2,1,0:T(8,128)S(1)}, f32[257,8,128]{2,1,0:T(8,128)}, u32[]{:S(2)}) copy-start(f32[257,8,128]{2,1,0:T(8,128)} %copy-done) | copy-start | bytes 3158020
  82.9 0.8 copy-start.6
  83.7 0.8 copy-start.8
  84.5 14.4 %collective-permute-start.9 = (f32[128,8,128]{2,1,0:T(8,128)}, f32[128,8,128]{2,1,0:T(8,128)}, u32[]{:S(2)}, u32[]{:S(2)}) collective-permute-start(f32[128,8,128]{2,1,0:T(8,128)} %get-tuple-element.24), channel_id=1, source_target_pairs={{0,3},{1,126},{2,5},{3,0},{4,7},{5,2},{6,9},{7,4},{8,11},{9,6},{10... | collective-permute-start | bytes 1572872 | tf_op jit(solution)/shard_map/ppermute | solution.py:248
  84.5 32.6 %collective-permute-start.7 = (f32[128,8,128]{2,1,0:T(8,128)}, f32[128,8,128]{2,1,0:T(8,128)}, u32[]{:S(2)}, u32[]{:S(2)}) collective-permute-start(f32[128,8,128]{2,1,0:T(8,128)} %get-tuple-element.18), channel_id=1, source_target_pairs={{0,2},{1,127},{2,4},{3,1},{4,6},{5,3},{6,8},{7,5},{8,10},{9,7},{10... | collective-permute-start | bytes 1572872 | tf_op jit(solution)/shard_map/ppermute | solution.py:248
  98.8 1.0 copy-start.5
  99.9 1.0 copy-start.9
  100.9 16.2 %copy-start.7 = (f32[128,8,128]{2,1,0:T(8,128)S(1)}, f32[128,8,128]{2,1,0:T(8,128)}, u32[]{:S(2)}) copy-start(f32[128,8,128]{2,1,0:T(8,128)} %copy-done.6) | copy-start | bytes 1572868

commit v2 on v1

v2 whole, which is shorter than its diff:
```python
import functools

import jax
import jax.numpy as jnp
from jax import lax
from jax.experimental import pallas as pl
from jax.experimental.pallas import tpu as pltpu
from jax.sharding import PartitionSpec as P

SUBSTEPS = 4

growth_rate = 1.0
quartic_rate = 1.0
coupling = 1.5
gradient_energy = 2.0
time_step = 0.02

HALF_BLOCKS = 128
PIECE = (HALF_BLOCKS, 8, 128)
TILE = (2, 64, 4, 8, 128)


META = 2 * HALF_BLOCKS
BOX_BLOCKS = (8, 32, 8, 128)
PADDED = (34, 80, 128)


def load_metas(refs, metas, sems, at=META):
    copies = [
        pltpu.make_async_copy(ref.at[META if n else at], metas.at[n], sems.at[n]) for n, ref in enumerate(refs)
    ]
    for copy in copies:
        copy.start()
    for copy in copies:
        copy.wait()


def number(metas, who, index):
    return metas[who, 0, index].astype(jnp.int32)


def box_meta(metas, who, slot, flip):
    first = slot == 0
    offset = jnp.where(first, number(metas, who, 0), number(metas, who, 1))
    row = jnp.where(first, number(metas, who, 2), number(metas, who, 3)) & 3
    column = jnp.where(first, number(metas, who, 4), number(metas, who, 5)) & 3
    return jnp.where(flip == 1, -offset, offset), row, column


def inbound(metas, who, flip):
    return jnp.where(flip == 1, number(metas, who, 7), number(metas, who, 6)) & 1


def deposit(tile_ref, piece_ref, base, row, column):
    lane = lax.broadcasted_iota(jnp.int32, (8, 128), 1)
    inside = ((lane - 32 * column) & 127) < 64
    shift = 32 * column
    shift_odd = (32 * column + 64) & 127

    def body(step, carry):
        for sub in range(4):
            m = step * 4 + sub
            place = (16 * row + m) & 63
            for it in range(4):
                value = piece_ref[base + it * 32 + m]
                value = value * value
                even = jnp.where(inside, pltpu.roll(value, shift, 1), 0.0)
                odd = jnp.where(inside, pltpu.roll(value, shift_odd, 1), 0.0)
                tile_ref[0, place, it] += even
                tile_ref[1, place, it] += odd
        return carry

    lax.fori_loop(0, 8, body, 0)


def extract(tile_ref, out_ref, row, column):
    lane = lax.broadcasted_iota(jnp.int32, (8, 128), 1)
    low = lane < 64
    shift = (128 - 32 * column) & 127
    shift_odd = (192 - 32 * column) & 127

    def body(step, carry):
        for sub in range(4):
            m = step * 4 + sub
            place = (16 * row + m) & 63
            for it in range(4):
                even = pltpu.roll(tile_ref[0, place, it], shift, 1)
                odd = pltpu.roll(tile_ref[1, place, it], shift_odd, 1)
                out_ref[it * 32 + m] = jnp.where(low, even, odd)
        return carry

    lax.fori_loop(0, 8, body, 0)


def deposit_if(cond, tile_ref, piece_ref, slot, row, column):
    @pl.when(cond)
    def _():
        deposit(tile_ref, piece_ref, slot * HALF_BLOCKS, row, column)


def clear(tile_ref):
    def body(step, carry):
        for sub in range(4):
            for par in range(2):
                for it in range(4):
                    tile_ref[par, step * 4 + sub, it] = jnp.zeros((8, 128), jnp.float32)
        return carry

    lax.fori_loop(0, 16, body, 0)


def message_kernel(boxes, anchors_hbm, migrations_hbm, outer, inner, anchors, migrations, sem):
    position = lax.axis_index("dev")
    devices = lax.axis_size("dev")
    flip = position & 1
    small = [
        pltpu.make_async_copy(anchors_hbm, anchors, sem.at[16]),
        pltpu.make_async_copy(migrations_hbm, migrations, sem.at[17]),
    ]
    copies = []
    for message, first in ((outer, 4 * flip), (inner, 4 - 4 * flip)):
        for box in range(2):
            for it in range(4):
                at = pl.ds(box * HALF_BLOCKS + it * 32, 32)
                copies.append(
                    pltpu.make_async_copy(boxes.at[box, first + it], message.at[at], sem.at[len(copies)])
                )
    for copy in small + copies:
        copy.start()
    for copy in small:
        copy.wait()
    lane = lax.broadcasted_iota(jnp.int32, (8, 128), 1)
    values = []
    for box in range(2):
        ahead = anchors[box, 0] - position + 1
        ahead = jnp.where(ahead < 0, ahead + devices, ahead)
        values.append(jnp.where(ahead >= devices, ahead - devices, ahead) - 1)
    values += [anchors[box, axis] for axis in (1, 2) for box in range(2)]
    values += [migrations[0, 0], migrations[0, 1]]
    block = jnp.zeros((8, 128), jnp.int32)
    for index, value in enumerate(values):
        block = jnp.where(lane == index, value, block)
    block = block.astype(jnp.float32)
    outer[META] = block
    inner[META] = block
    for copy in copies:
        copy.wait()


def local_kernel(mine_outer, mine_inner, sib_outer, sib_inner, tile_0, tile_1, metas, sems):
    load_metas((mine_outer, sib_outer), metas, sems)
    flip = lax.axis_index("dev") & 1
    clear(tile_0)
    clear(tile_1)
    for slot in range(2):
        u, row, column = box_meta(metas, 0, slot, flip)
        deposit_if(u == 0, tile_0, mine_outer, slot, row, column)
        deposit_if(u == -1, tile_0, mine_inner, slot, row, column)
        deposit_if(u == 1, tile_1, mine_outer, slot, row, column)
        deposit_if(u == 0, tile_1, mine_inner, slot, row, column)
        u, row, column = box_meta(metas, 1, slot, flip)
        deposit_if(u == -1, tile_0, sib_inner, slot, row, column)
        deposit_if(u == 0, tile_1, sib_inner, slot, row, column)
        deposit_if(u == -1, tile_1, sib_outer, slot, row, column)


def inner_kernel(part, sib_outer, out_outer, beyond,
                 to_next, window_out, window_sib, tile, metas, sems):
    copy = pltpu.make_async_copy(part, tile, sems.at[3])
    copy.start()
    load_metas((sib_outer, out_outer, beyond), metas, sems)
    copy.wait()
    flip = lax.axis_index("dev") & 1
    for slot in range(2):
        u, row, column = box_meta(metas, 1, slot, flip)
        deposit_if(u == 1, tile, out_outer, slot, row, column)
        u, row, column = box_meta(metas, 2, slot, flip)
        deposit_if(u == -1, tile, beyond, slot, row, column)
    leaving = inbound(metas, 0, flip)
    _, row, column = box_meta(metas, 0, leaving, flip)
    extract(tile, to_next.at[:HALF_BLOCKS], row, column)
    _, row, column = box_meta(metas, 2, inbound(metas, 2, flip), flip)
    extract(tile, to_next.at[HALF_BLOCKS:], row, column)
    _, row, column = box_meta(metas, 1, inbound(metas, 1, flip), flip)
    extract(tile, window_out, row, column)
    _, row, column = box_meta(metas, 0, 1 - leaving, flip)
    extract(tile, window_sib, row, column)


def outer_kernel(part, mine_outer, sib_outer, out_outer, out_inners,
                 to_next, to_sib, window_out, window_sib, tile, metas, sems):
    copy = pltpu.make_async_copy(part, tile, sems.at[4])
    copy.start()
    load_metas((out_inners, out_outer, sib_outer, mine_outer), metas, sems, 2 * META + 1)
    copy.wait()
    flip = lax.axis_index("dev") & 1
    for slot in range(2):
        u, row, column = box_meta(metas, 1, slot, flip)
        deposit_if(u == 0, tile, out_outer, slot, row, column)
        deposit_if(u == 1, tile, out_inners, slot, row, column)
        u, row, column = box_meta(metas, 0, slot, flip)

        @pl.when(u == 1)
        def _(slot=slot, row=row, column=column):
            deposit(tile, out_inners, META + 1 + slot * HALF_BLOCKS, row, column)

    leaving = inbound(metas, 2, flip)
    _, row, column = box_meta(metas, 2, leaving, flip)
    extract(tile, to_next, row, column)
    _, row, column = box_meta(metas, 3, inbound(metas, 3, flip), flip)
    extract(tile, to_sib, row, column)
    _, row, column = box_meta(metas, 1, inbound(metas, 1, flip), flip)
    extract(tile, window_out, row, column)
    _, row, column = box_meta(metas, 2, 1 - leaving, flip)
    extract(tile, window_sib, row, column)


def substep(source, factor, store, first, last, width):
    shape = (8, 128)
    lane = lax.broadcasted_iota(jnp.int32, shape, 1)
    low = lane < 64
    last_z = (lane & 63) == 63
    first_z = (lane & 63) == 0

    def body(step, carry):
        for sub in range(width):
            m = step * width + sub
            for it in range(8):
                row = 8 + 8 * it
                value = source[m + 1, row:row + 8]
                beside = source[m + 1, row + 1:row + 9] + source[m + 1, row - 1:row + 7]
                lines = jnp.where(low, source[m + 2, row:row + 8], source[m, row:row + 8])
                beside += pltpu.roll(value + lines, 64, 1)
                beside += jnp.where(last_z, 0.0, pltpu.roll(value, 127, 1))
                beside += jnp.where(first_z, 0.0, pltpu.roll(value, 1, 1))
                rate = factor[m, 8 * it:8 * it + 8] - (time_step * quartic_rate) * (value * value)
                store(m, it, value * rate + (time_step * gradient_energy) * beside)
        return carry

    lax.fori_loop(first // width, last // width, body, 0)


def relax_kernel(half_0, half_1, mine_outer, *refs, first):
    windows, result_hbm, (result, factor, ping, pong, metas, sems) = refs[:4], refs[-7], refs[-6:]
    load_metas((half_1, mine_outer), metas, sems)
    flip = lax.axis_index("dev") & 1
    slot = inbound(metas, 0, flip) if first < 0 else 1 - inbound(metas, 0, flip)
    own_slot = inbound(metas, 1, flip)
    own_slot = own_slot if first < 0 else 1 - own_slot
    u, _, _ = box_meta(metas, 0, slot, flip)
    base = 1.0 + time_step * (growth_rate - 6.0 * gradient_energy)
    scale = 2.0 * coupling * time_step

    for buffer in (ping, pong):
        for at in (0, 33):
            buffer[at] = jnp.zeros(PADDED[1:], jnp.float32)
        for m in range(1, 33):
            buffer[m, 0:8] = jnp.zeros((8, 128), jnp.float32)
            buffer[m, 72:80] = jnp.zeros((8, 128), jnp.float32)

    for g, half in ((0, half_0), (1, half_1)):
        at = jnp.where(flip == 1, 1 - g, g) * 32
        tile = first + u + g
        for index, window in enumerate(windows):
            @pl.when(tile == first - 1 + index)
            def _(window=window, half=half, at=at):
                def body(step, carry):
                    for sub in range(4):
                        m = step * 4 + sub
                        for it in range(4):
                            value = half[slot * HALF_BLOCKS + it * 32 + m]
                            rows = pl.multiple_of(at + 8 * it, 8)
                            ping[m + 1, pl.ds(pl.multiple_of(rows + 8, 8), 8)] = value
                            others = window[it * 32 + m] - value * value
                            factor[m, pl.ds(rows, 8)] = base - scale * others
                    return carry

                lax.fori_loop(0, 8, body, 0)

    def to(buffer):
        def store(m, it, value):
            buffer[m + 1, 8 + 8 * it:16 + 8 * it] = value

        return store

    def to_result(m, it, value):
        result[it, m] = value

    substep(ping, factor, to(pong), 0, 32, 8)
    substep(pong, factor, to(ping), 0, 32, 8)
    substep(ping, factor, to(pong), 0, 32, 8)
    copies = []
    for part in range(2):
        substep(pong, factor, to_result, 16 * part, 16 * part + 16, 8)
        lines = pl.ds(16 * part, 16)
        copy = pltpu.make_async_copy(
            result.at[:, lines], result_hbm.at[own_slot, :, lines], sems.at[2 + part]
        )
        copy.start()
        copies.append(copy)
    for copy in copies:
        copy.wait()


def on_device(grain_boxes, box_anchors, migrations):
    devices = lax.axis_size("dev")
    chips = devices // 2

    def pairs_of(even_step, odd_step):
        pairs = []
        for chip in range(chips):
            pairs.append((2 * chip, (2 * chip + even_step) % devices))
            pairs.append((2 * chip + 1, (2 * chip + 1 + odd_step) % devices))
        return pairs

    sibling, outward = pairs_of(1, -1), pairs_of(-1, 1)
    inward = pairs_of(2, -2)

    def send(value, pairs):
        return lax.ppermute(value, "dev", pairs)

    boxes = grain_boxes.reshape(2, 8, 8, 32, 128).transpose(0, 1, 3, 2, 4)

    vmem = pl.BlockSpec(memory_space=pltpu.VMEM)
    anywhere = pl.BlockSpec(memory_space=pl.ANY)
    params = pltpu.CompilerParams(vmem_limit_bytes=48 << 20)
    message_type = jax.ShapeDtypeStruct((2 * HALF_BLOCKS + 1, 8, 128), jnp.float32)
    tile_type = jax.ShapeDtypeStruct(TILE, jnp.float32)
    piece_type = jax.ShapeDtypeStruct(PIECE, jnp.float32)

    def metas(count, sems):
        return [pltpu.SMEM((count, 8, 128), jnp.float32), pltpu.SemaphoreType.DMA((sems,))]

    outer, inner = pl.pallas_call(
        message_kernel,
        in_specs=[pl.BlockSpec(memory_space=pltpu.HBM)] * 3,
        out_specs=[vmem] * 2,
        out_shape=[message_type] * 2,
        scratch_shapes=[
            pltpu.SMEM((2, 3), jnp.int32),
            pltpu.SMEM((1, 2), jnp.int32),
            pltpu.SemaphoreType.DMA((18,)),
        ],
        compiler_params=params,
        name="messages",
    )(*(pltpu.with_memory_space_constraint(a, pltpu.HBM) for a in (boxes, box_anchors, migrations)))

    out_outer = send(outer, outward)
    sib_outer = send(outer, sibling)
    sib_inner = send(inner, sibling)
    out_inners = send(jnp.concatenate([inner, sib_inner]), outward)

    part_0, part_1 = pl.pallas_call(
        local_kernel,
        in_specs=[vmem] * 4,
        out_specs=[vmem] * 2,
        out_shape=[tile_type] * 2,
        scratch_shapes=metas(2, 2),
        compiler_params=params,
        name="local_tiles",
    )(outer, inner, sib_outer, sib_inner)

    out_outer, part_1 = lax.optimization_barrier((out_outer, part_1))
    beyond = send(out_outer, sibling)

    tile_scratch = [pltpu.VMEM(TILE, jnp.float32)]
    to_next, window_out_1, window_sib_1 = pl.pallas_call(
        inner_kernel,
        in_specs=[anywhere] + [vmem] * 3,
        out_specs=[vmem] * 3,
        out_shape=[jax.ShapeDtypeStruct((META, 8, 128), jnp.float32)] + [piece_type] * 2,
        scratch_shapes=tile_scratch + metas(3, 4),
        compiler_params=params,
        name="inner_tile",
    )(part_1, sib_outer, out_outer, beyond)
    near = send(to_next, inward)

    part_0, window_out_1 = lax.optimization_barrier((part_0, window_out_1))
    to_next, to_sib, window_out_0, window_sib_0 = pl.pallas_call(
        outer_kernel,
        in_specs=[anywhere] + [vmem] * 4,
        out_specs=[vmem] * 4,
        out_shape=[piece_type] * 4,
        scratch_shapes=tile_scratch + metas(4, 5),
        compiler_params=params,
        name="outer_tile",
    )(part_0, outer, sib_outer, out_outer, out_inners)
    far_out = send(to_next, inward)
    from_sib = send(to_sib, sibling)
    near, window_out_0 = lax.optimization_barrier((near, window_out_0))
    near_sib = send(near[HALF_BLOCKS:], sibling)

    def relax(name, first, halves, windows, held):
        return pl.pallas_call(
            functools.partial(relax_kernel, first=first),
            in_specs=[vmem] * 7 + [anywhere] * len(held),
            out_specs=anywhere,
            out_shape=jax.ShapeDtypeStruct((2,) + BOX_BLOCKS, jnp.float32),
            scratch_shapes=[
                pltpu.VMEM(BOX_BLOCKS, jnp.float32),
                pltpu.VMEM((32, 64, 128), jnp.float32),
                pltpu.VMEM(PADDED, jnp.float32),
                pltpu.VMEM(PADDED, jnp.float32),
            ] + metas(2, 4),
            input_output_aliases={7: 0} if held else {},
            compiler_params=params,
            name=name,
        )(*halves, outer, *windows, *held)

    held = relax(
        "relax_sibling", 1, (sib_inner, sib_outer),
        (window_sib_0, window_sib_1, from_sib, near_sib), (),
    )
    relaxed = relax(
        "relax_outer", -1, (out_inners, out_outer),
        (far_out, near, window_out_0, window_out_1), (held,),
    )
    return relaxed.transpose(0, 1, 3, 2, 4).reshape(grain_boxes.shape)


def solution(mesh):
    in_specs = (P("dev", None, None), P("dev", None), P("dev", None))
    out_specs = P("dev", None, None)
    return jax.shard_map(
        on_device, mesh=mesh, in_specs=in_specs, out_specs=out_specs, check_vma=False
    )
```

time: 134 us -> 85.6 us (0.64)
  Pallas kernels: 71.1 us -> 33.6 us
  waiting for transfers between devices: 5.01 us -> 17.1 us
  local copies, waits for them, and re-layouts: 10.2 us -> 1.36 us
  between operations: 6.83 us -> 0.06 us
  other arithmetic: 5 us -> 0.14 us
  starting transfers between devices: 35.1 us -> 32.3 us
    pallas_call x5 -> x6, Pallas kernels: 71.1 us -> 33.6 us  [the longest x2 14.1 us: relax(): pl.pallas_call(functools.partial(relax_kernel, first=first), in_specs=[vm...]
    ppermute x10 -> x9, waiting for transfers between devices: 5.01 us -> 17.1 us  [send(): return lax.ppermute(value, 'dev', pairs)]
    dynamic_slice x5 -> x0, local copies, waits for them, and re-layouts: 3.24 us -> none  [the longest x2 1.32 us: numbers(): slot = values[sign_slot]]
    unnamed x22 -> x2, local copies, waits for them, and re-layouts: 4.49 us -> 1.33 us
    ppermute x10 -> x9, starting transfers between devices: 35.1 us -> 32.3 us  [send(): return lax.ppermute(value, 'dev', pairs)]
    another operation x2 -> x0, other arithmetic: 2.78 us -> none  [numbers(): jnp.stack([slot, parity, jnp.where(parity == 1, -offset, offset), own_slot])]
    another operation x1 -> x0, local copies, waits for them, and re-layouts: 1.69 us -> none
  transfers between devices with their start and end apart: 10 -> 9, of which waited for: 3 -> 5; matrix products, arithmetic and copies ran while one was open for 5% -> 0% of each run, Pallas kernels for 41% -> 28%
where the time goes in v2:
time: 85.6 us; the launch traced here: 84.5 us
  Pallas kernels  33.6 us (39%)
  starting transfers between devices  32.3 us (38%)
  waiting for transfers between devices  17.1 us (20%)
  local copies, waits for them, and re-layouts  1.36 us (2%)
    ppermute x9, starting transfers between devices, send(): return lax.ppermute(value, 'dev', pairs)  32.3 us
    ppermute x9, waiting for transfers between devices, send(): return lax.ppermute(value, 'dev', pairs)  17.1 us
    pallas_call x2, Pallas kernels, relax(): pl.pallas_call(functools.partial(relax_kernel, first=first), in_specs=[vm...  14.1 us
    pallas_call x1, Pallas kernels, on_device(): pl.pallas_call(outer_kernel, in_specs=[anywhere] + [vmem] * 4, out_specs=...  7.3 us
    pallas_call x1, Pallas kernels, on_device(): pl.pallas_call(inner_kernel, in_specs=[anywhere] + [vmem] * 3, out_specs=...  5.7 us
    pallas_call x1, Pallas kernels, on_device(): pl.pallas_call(local_kernel, in_specs=[vmem] * 4, out_specs=[vmem] * 2, o...  4.77 us
    pallas_call x1, Pallas kernels, on_device(): pl.pallas_call(message_kernel, in_specs=[pl.BlockSpec(memory_space=pltpu....  1.75 us
  transfers between devices with their start and end apart: 9, of which 5 were waited for; matrix products, arithmetic and copies ran while one was open for 0% of the time, Pallas kernels for 28%

profile of v2, /device:TPU:1, one launch (start us, length us, event | category | flops | bytes accessed | tf_op | source)
XLA Modules:
  0.0 84.5 jit_solution(11271090304780319937)
XLA Ops:
  0.0 1.8 %messages.1 = (f32[257,8,128]{2,1,0:T(8,128)S(1)}, f32[257,8,128]{2,1,0:T(8,128)S(1)}) custom-call(f32[2,8,32,8,128]{4,3,2,1,0:T(8,128)} %bitcast.6, s32[2,3]{1,0:T(2,128)} %anchors_hbm.1, s32[1,2]{1,0:T(1,128)} %migrations_hbm.1), custom_call_target="tpu_custom_call" | custom-call | tf_op jit(solution)/shard_map/messages/pallas_call | solution.py:334
  1.8 1.5 %collective-permute-start = (f32[257,8,128]{2,1,0:T(8,128)S(1)}, f32[257,8,128]{2,1,0:T(8,128)S(1)}, u32[]{:S(2)}, u32[]{:S(2)}) collective-permute-start(f32[257,8,128]{2,1,0:T(8,128)S(1)} %get-tuple-element.22.mine_inner), channel_id=1, source_target_pairs={{0,1},{1,0},{2,3},{3,2},{4,5},{5,4},{6,7},{7,6},{8,9},{9,8},{10,11... | collective-permute-start | bytes 3158024 | tf_op jit(solution)/shard_map/ppermute | solution.py:320
  3.3 0.1 collective-permute-start.3
  3.4 1.7 %collective-permute-start.2 = (f32[257,8,128]{2,1,0:T(8,128)S(1)}, f32[257,8,128]{2,1,0:T(8,128)S(1)}, u32[]{:S(2)}, u32[]{:S(2)}) collective-permute-start(f32[257,8,128]{2,1,0:T(8,128)S(1)} %get-tuple-element.23.mine_outer), channel_id=1, source_target_pairs={{0,127},{1,2},{2,1},{3,4},{4,3},{5,6},{6,5},{7,8},{8,7},{9,10},{10... | collective-permute-start | bytes 3158024 | tf_op jit(solution)/shard_map/ppermute | solution.py:320
  5.0 0.5 collective-permute-done.sib_inner.half_0
  5.6 0.1 pad_maximum_fusion
  5.7 1.7 %collective-permute-start.1 = (f32[514,8,128]{2,1,0:T(8,128)S(1)}, f32[514,8,128]{2,1,0:T(8,128)S(1)}, u32[]{:S(2)}, u32[]{:S(2)}) collective-permute-start(f32[514,8,128]{2,1,0:T(8,128)S(1)} %pad_maximum_fusion), channel_id=1, source_target_pairs={{0,127},{1,2},{2,1},{3,4},{4,3},{5,6},{6,5},{7,8},{8,7},{9,10},{10... | collective-permute-start | bytes 6316040 | tf_op jit(solution)/shard_map/ppermute | solution.py:320
  7.4 0.0 collective-permute-done.3.sib_outer.half_1
  7.4 4.8 %local_tiles.1 = (f32[2,64,4,8,128]{4,3,2,1,0:T(8,128)}, f32[2,64,4,8,128]{4,3,2,1,0:T(8,128)}) custom-call(f32[257,8,128]{2,1,0:T(8,128)S(1)} %get-tuple-element.23.mine_outer, f32[257,8,128]{2,1,0:T(8,128)S(1)} %get-tuple-element.22.mine_inner, f32[257,8,128]{2,1,0:T(8,128)S(1)} %collective-permute-done.3.sib_outer.half_1, ...), custom_call_target="tpu_custom_call" | custom-call | tf_op jit(solution)/shard_map/local_tiles/pallas_call | solution.py:353
  12.2 5.7 %collective-permute-done.2.out_outer.half_1 = f32[257,8,128]{2,1,0:T(8,128)S(1)} collective-permute-done((f32[257,8,128]{2,1,0:T(8,128)S(1)}, f32[257,8,128]{2,1,0:T(8,128)S(1)}, u32[]{:S(2)}, u32[]{:S(2)}) %collective-permute-start.2) | collective-permute-done | bytes 1052704 | tf_op jit(solution)/shard_map/ppermute | solution.py:320
  17.9 6.8 %collective-permute-start.4 = (f32[257,8,128]{2,1,0:T(8,128)S(1)}, f32[257,8,128]{2,1,0:T(8,128)S(1)}, u32[]{:S(2)}, u32[]{:S(2)}) collective-permute-start(f32[257,8,128]{2,1,0:T(8,128)S(1)} %collective-permute-done.2.out_outer.half_1), channel_id=1, source_target_pairs={{0,1},{1,0},{2,3},{3,2},{4,5},{5,4},{6,7},{7,6},{8,9},{9,8},{10,11... | collective-permute-start | bytes 3158024 | tf_op jit(solution)/shard_map/ppermute | solution.py:320
  24.8 2.3 %collective-permute-done.4.beyond = f32[257,8,128]{2,1,0:T(8,128)S(1)} collective-permute-done((f32[257,8,128]{2,1,0:T(8,128)S(1)}, f32[257,8,128]{2,1,0:T(8,128)S(1)}, u32[]{:S(2)}, u32[]{:S(2)}) %collective-permute-start.4) | collective-permute-done | bytes 1052704 | tf_op jit(solution)/shard_map/ppermute | solution.py:320
  27.1 5.7 %inner_tile.1 = (f32[256,8,128]{2,1,0:T(8,128)S(1)}, f32[128,8,128]{2,1,0:T(8,128)S(1)}, f32[128,8,128]{2,1,0:T(8,128)S(1)}) custom-call(f32[2,64,4,8,128]{4,3,2,1,0:T(8,128)} %get-tuple-element.27.part, f32[257,8,128]{2,1,0:T(8,128)S(1)} %collective-permute-done.3.sib_outer.half_1, f32[257,8,128]{2,1,0:T(8,128)S(1)} %collective-permute-done.2.out_outer.half_1, ...), custom_call_target="tpu_custom_call" | custom-call | tf_op jit(solution)/shard_map/inner_tile/pallas_call | solution.py:367
  32.8 8.1 %collective-permute-start.6 = (f32[256,8,128]{2,1,0:T(8,128)S(1)}, f32[256,8,128]{2,1,0:T(8,128)S(1)}, u32[]{:S(2)}, u32[]{:S(2)}) collective-permute-start(f32[256,8,128]{2,1,0:T(8,128)S(1)} %get-tuple-element.31), channel_id=1, source_target_pairs={{0,2},{1,127},{2,4},{3,1},{4,6},{5,3},{6,8},{7,5},{8,10},{9,7},{10... | collective-permute-start | bytes 3145736 | tf_op jit(solution)/shard_map/ppermute | solution.py:320
  40.8 4.5 %collective-permute-done.1.out_inners.half_0 = f32[514,8,128]{2,1,0:T(8,128)S(1)} collective-permute-done((f32[514,8,128]{2,1,0:T(8,128)S(1)}, f32[514,8,128]{2,1,0:T(8,128)S(1)}, u32[]{:S(2)}, u32[]{:S(2)}) %collective-permute-start.1) | collective-permute-done | bytes 2105376 | tf_op jit(solution)/shard_map/ppermute | solution.py:320
  45.3 0.0 copy-start
  45.3 1.3 %copy-done = f32[514,8,128]{2,1,0:T(8,128)} copy-done((f32[514,8,128]{2,1,0:T(8,128)}, f32[514,8,128]{2,1,0:T(8,128)S(1)}, u32[]{:S(2)}) %copy-start) | copy-done | bytes 2105368
  46.7 7.3 %outer_tile.1 = (f32[128,8,128]{2,1,0:T(8,128)S(1)}, f32[128,8,128]{2,1,0:T(8,128)S(1)}, f32[128,8,128]{2,1,0:T(8,128)S(1)}, f32[128,8,128]{2,1,0:T(8,128)S(1)}) custom-call(f32[2,64,4,8,128]{4,3,2,1,0:T(8,128)} %get-tuple-element.29.part, f32[257,8,128]{2,1,0:T(8,128)S(1)} %get-tuple-element.23.mine_outer, ...), custom_call_target="tpu_custom_call" | custom-call | tf_op jit(solution)/shard_map/outer_tile/pallas_call | solution.py:379
  54.0 4.0 %collective-permute-done.6.refs_1_ = f32[256,8,128]{2,1,0:T(8,128)S(1)} collective-permute-done((f32[256,8,128]{2,1,0:T(8,128)S(1)}, f32[256,8,128]{2,1,0:T(8,128)S(1)}, u32[]{:S(2)}, u32[]{:S(2)}) %collective-permute-start.6) | collective-permute-done | bytes 1048608 | tf_op jit(solution)/shard_map/ppermute | solution.py:320
  58.0 5.7 %collective-permute-start.8 = (f32[128,8,128]{2,1,0:T(8,128)S(1)}, f32[128,8,128]{2,1,0:T(8,128)S(1)}, u32[]{:S(2)}, u32[]{:S(2)}) collective-permute-start(f32[128,8,128]{2,1,0:T(8,128)S(1)} %slice.3), channel_id=1, source_target_pairs={{0,1},{1,0},{2,3},{3,2},{4,5},{5,4},{6,7},{7,6},{8,9},{9,8},{10,11... | collective-permute-start | bytes 1572872 | tf_op jit(solution)/shard_map/ppermute | solution.py:320
  63.8 0.1 collective-permute-start.7
  63.9 6.5 %collective-permute-start.5 = (f32[128,8,128]{2,1,0:T(8,128)S(1)}, f32[128,8,128]{2,1,0:T(8,128)S(1)}, u32[]{:S(2)}, u32[]{:S(2)}) collective-permute-start(f32[128,8,128]{2,1,0:T(8,128)S(1)} %get-tuple-element.30), channel_id=1, source_target_pairs={{0,2},{1,127},{2,4},{3,1},{4,6},{5,3},{6,8},{7,5},{8,10},{9,7},{10... | collective-permute-start | bytes 1572872 | tf_op jit(solution)/shard_map/ppermute | solution.py:320
  70.4 0.0 collective-permute-done.8.refs_3_
  70.4 0.0 collective-permute-done.7.refs_2_
  70.4 6.3 %relax_sibling.1.refs_4_ = f32[2,8,32,8,128]{4,3,2,1,0:T(8,128)} custom-call(f32[257,8,128]{2,1,0:T(8,128)S(1)} %collective-permute-done.sib_inner.half_0, f32[257,8,128]{2,1,0:T(8,128)S(1)} %collective-permute-done.3.sib_outer.half_1, f32[257,8,128]{2,1,0:T(8,128)S(1)} %get-tuple-element.23.mine_outer, f32[128,8,128]{2,1,0:T(8,128)S(1)} %get-tuple-element.36.refs_0_, ...), custom_call_target="tpu_custom_call" | custom-call | tf_op jit(solution)/shard_map/relax_sibling/pallas_call | solution.py:394
  76.7 0.0 collective-permute-done.5.refs_0_
  76.7 7.8 %relax_outer.1 = f32[2,8,32,8,128]{4,3,2,1,0:T(8,128)} custom-call(f32[514,8,128]{2,1,0:T(8,128)} %copy-done, f32[257,8,128]{2,1,0:T(8,128)S(1)} %collective-permute-done.2.out_outer.half_1, f32[257,8,128]{2,1,0:T(8,128)S(1)} %get-tuple-element.23.mine_outer, f32[128,8,128]{2,1,0:T(8,128)S(1)} %collective-permute-done.5.refs_0_, ...), custom_call_target="tpu_custom_call", output_to_operand_aliasing={{}: (7, {})} | custom-call | tf_op jit(solution)/shard_map/relax_outer/pallas_call | solution.py:394
  (1 shorter events, 0.0 us)
Async XLA Ops:
  1.8 3.8 %collective-permute-start = (f32[257,8,128]{2,1,0:T(8,128)S(1)}, f32[257,8,128]{2,1,0:T(8,128)S(1)}, u32[]{:S(2)}, u32[]{:S(2)}) collective-permute-start(f32[257,8,128]{2,1,0:T(8,128)S(1)} %get-tuple-element.22.mine_inner), channel_id=1, source_target_pairs={{0,1},{1,0},{2,3},{3,2},{4,5},{5,4},{6,7},{7,6},{8,9},{9,8},{10,11... | collective-permute-start | bytes 3158024 | tf_op jit(solution)/shard_map/ppermute | solution.py:320
  3.3 4.2 %collective-permute-start.3 = (f32[257,8,128]{2,1,0:T(8,128)S(1)}, f32[257,8,128]{2,1,0:T(8,128)S(1)}, u32[]{:S(2)}, u32[]{:S(2)}) collective-permute-start(f32[257,8,128]{2,1,0:T(8,128)S(1)} %get-tuple-element.23.mine_outer), channel_id=1, source_target_pairs={{0,1},{1,0},{2,3},{3,2},{4,5},{5,4},{6,7},{7,6},{8,9},{9,8},{10,11... | collective-permute-start | bytes 3158024 | tf_op jit(solution)/shard_map/ppermute | solution.py:320
  3.4 14.6 %collective-permute-start.2 = (f32[257,8,128]{2,1,0:T(8,128)S(1)}, f32[257,8,128]{2,1,0:T(8,128)S(1)}, u32[]{:S(2)}, u32[]{:S(2)}) collective-permute-start(f32[257,8,128]{2,1,0:T(8,128)S(1)} %get-tuple-element.23.mine_outer), channel_id=1, source_target_pairs={{0,127},{1,2},{2,1},{3,4},{4,3},{5,6},{6,5},{7,8},{8,7},{9,10},{10... | collective-permute-start | bytes 3158024 | tf_op jit(solution)/shard_map/ppermute | solution.py:320
  5.7 39.6 %collective-permute-start.1 = (f32[514,8,128]{2,1,0:T(8,128)S(1)}, f32[514,8,128]{2,1,0:T(8,128)S(1)}, u32[]{:S(2)}, u32[]{:S(2)}) collective-permute-start(f32[514,8,128]{2,1,0:T(8,128)S(1)} %pad_maximum_fusion), channel_id=1, source_target_pairs={{0,127},{1,2},{2,1},{3,4},{4,3},{5,6},{6,5},{7,8},{8,7},{9,10},{10... | collective-permute-start | bytes 6316040 | tf_op jit(solution)/shard_map/ppermute | solution.py:320
  17.9 9.1 %collective-permute-start.4 = (f32[257,8,128]{2,1,0:T(8,128)S(1)}, f32[257,8,128]{2,1,0:T(8,128)S(1)}, u32[]{:S(2)}, u32[]{:S(2)}) collective-permute-start(f32[257,8,128]{2,1,0:T(8,128)S(1)} %collective-permute-done.2.out_outer.half_1), channel_id=1, source_target_pairs={{0,1},{1,0},{2,3},{3,2},{4,5},{5,4},{6,7},{7,6},{8,9},{9,8},{10,11... | collective-permute-start | bytes 3158024 | tf_op jit(solution)/shard_map/ppermute | solution.py:320
  32.8 25.2 %collective-permute-start.6 = (f32[256,8,128]{2,1,0:T(8,128)S(1)}, f32[256,8,128]{2,1,0:T(8,128)S(1)}, u32[]{:S(2)}, u32[]{:S(2)}) collective-permute-start(f32[256,8,128]{2,1,0:T(8,128)S(1)} %get-tuple-element.31), channel_id=1, source_target_pairs={{0,2},{1,127},{2,4},{3,1},{4,6},{5,3},{6,8},{7,5},{8,10},{9,7},{10... | collective-permute-start | bytes 3145736 | tf_op jit(solution)/shard_map/ppermute | solution.py:320
  45.3 1.3 %copy-start = (f32[514,8,128]{2,1,0:T(8,128)}, f32[514,8,128]{2,1,0:T(8,128)S(1)}, u32[]{:S(2)}) copy-start(f32[514,8,128]{2,1,0:T(8,128)S(1)} %collective-permute-done.1.out_inners.half_0) | copy-start | bytes 6316036
  58.0 12.4 %collective-permute-start.8 = (f32[128,8,128]{2,1,0:T(8,128)S(1)}, f32[128,8,128]{2,1,0:T(8,128)S(1)}, u32[]{:S(2)}, u32[]{:S(2)}) collective-permute-start(f32[128,8,128]{2,1,0:T(8,128)S(1)} %slice.3), channel_id=1, source_target_pairs={{0,1},{1,0},{2,3},{3,2},{4,5},{5,4},{6,7},{7,6},{8,9},{9,8},{10,11... | collective-permute-start | bytes 1572872 | tf_op jit(solution)/shard_map/ppermute | solution.py:320
  63.8 6.6 %collective-permute-start.7 = (f32[128,8,128]{2,1,0:T(8,128)S(1)}, f32[128,8,128]{2,1,0:T(8,128)S(1)}, u32[]{:S(2)}, u32[]{:S(2)}) collective-permute-start(f32[128,8,128]{2,1,0:T(8,128)S(1)} %get-tuple-element.38), channel_id=1, source_target_pairs={{0,1},{1,0},{2,3},{3,2},{4,5},{5,4},{6,7},{7,6},{8,9},{9,8},{10,11... | collective-permute-start | bytes 1572872 | tf_op jit(solution)/shard_map/ppermute | solution.py:320
  63.9 12.8 %collective-permute-start.5 = (f32[128,8,128]{2,1,0:T(8,128)S(1)}, f32[128,8,128]{2,1,0:T(8,128)S(1)}, u32[]{:S(2)}, u32[]{:S(2)}) collective-permute-start(f32[128,8,128]{2,1,0:T(8,128)S(1)} %get-tuple-element.30), channel_id=1, source_target_pairs={{0,2},{1,127},{2,4},{3,1},{4,6},{5,3},{6,8},{7,5},{8,10},{9,7},{10... | collective-permute-start | bytes 1572872 | tf_op jit(solution)/shard_map/ppermute | solution.py:320

commit v3 on v2

--- a/solution.py
+++ b/solution.py
@@ -58,8 +58,8 @@
     shift_odd = (32 * column + 64) & 127
 
     def body(step, carry):
-        for sub in range(4):
-            m = step * 4 + sub
+        for sub in range(16):
+            m = step * 16 + sub
             place = (16 * row + m) & 63
             for it in range(4):
                 value = piece_ref[base + it * 32 + m]
@@ -70,26 +70,27 @@
                 tile_ref[1, place, it] += odd
         return carry
 
-    lax.fori_loop(0, 8, body, 0)
-
-
-def extract(tile_ref, out_ref, row, column):
+    lax.fori_loop(0, 2, body, 0)
+
+
+def extract(tile_ref, out_refs, row, column):
     lane = lax.broadcasted_iota(jnp.int32, (8, 128), 1)
     low = lane < 64
     shift = (128 - 32 * column) & 127
     shift_odd = (192 - 32 * column) & 127
 
     def body(step, carry):
-        for sub in range(4):
-            m = step * 4 + sub
+        for sub in range(16):
+            m = step * 16 + sub
             place = (16 * row + m) & 63
             for it in range(4):
                 even = pltpu.roll(tile_ref[0, place, it], shift, 1)
                 odd = pltpu.roll(tile_ref[1, place, it], shift_odd, 1)
-                out_ref[it * 32 + m] = jnp.where(low, even, odd)
+                each = 4 // len(out_refs)
+                out_refs[it // each][it % each * 32 + m] = jnp.where(low, even, odd)
         return carry
 
-    lax.fori_loop(0, 8, body, 0)
+    lax.fori_loop(0, 2, body, 0)
 
 
 def deposit_if(cond, tile_ref, piece_ref, slot, row, column):
@@ -165,7 +166,7 @@
 
 
 def inner_kernel(part, sib_outer, out_outer, beyond,
-                 to_next, window_out, window_sib, tile, metas, sems):
+                 to_next, cross_0, cross_1, window_out, window_sib, tile, metas, sems):
     copy = pltpu.make_async_copy(part, tile, sems.at[3])
     copy.start()
     load_metas((sib_outer, out_outer, beyond), metas, sems)
@@ -178,17 +179,17 @@
         deposit_if(u == -1, tile, beyond, slot, row, column)
     leaving = inbound(metas, 0, flip)
     _, row, column = box_meta(metas, 0, leaving, flip)
-    extract(tile, to_next.at[:HALF_BLOCKS], row, column)
+    extract(tile, (to_next,), row, column)
     _, row, column = box_meta(metas, 2, inbound(metas, 2, flip), flip)
-    extract(tile, to_next.at[HALF_BLOCKS:], row, column)
+    extract(tile, (cross_0, cross_1), row, column)
     _, row, column = box_meta(metas, 1, inbound(metas, 1, flip), flip)
-    extract(tile, window_out, row, column)
+    extract(tile, (window_out,), row, column)
     _, row, column = box_meta(metas, 0, 1 - leaving, flip)
-    extract(tile, window_sib, row, column)
+    extract(tile, (window_sib,), row, column)
 
 
 def outer_kernel(part, mine_outer, sib_outer, out_outer, out_inners,
-                 to_next, to_sib, window_out, window_sib, tile, metas, sems):
+                 to_next, sib_0, sib_1, window_out, window_sib, tile, metas, sems):
     copy = pltpu.make_async_copy(part, tile, sems.at[4])
     copy.start()
     load_metas((out_inners, out_outer, sib_outer, mine_outer), metas, sems, 2 * META + 1)
@@ -206,42 +207,48 @@
 
     leaving = inbound(metas, 2, flip)
     _, row, column = box_meta(metas, 2, leaving, flip)
-    extract(tile, to_next, row, column)
+    extract(tile, (to_next,), row, column)
     _, row, column = box_meta(metas, 3, inbound(metas, 3, flip), flip)
-    extract(tile, to_sib, row, column)
+    extract(tile, (sib_0, sib_1), row, column)
     _, row, column = box_meta(metas, 1, inbound(metas, 1, flip), flip)
-    extract(tile, window_out, row, column)
+    extract(tile, (window_out,), row, column)
     _, row, column = box_meta(metas, 2, 1 - leaving, flip)
-    extract(tile, window_sib, row, column)
-
-
-def substep(source, factor, store, first, last, width):
-    shape = (8, 128)
-    lane = lax.broadcasted_iota(jnp.int32, shape, 1)
-    low = lane < 64
-    last_z = (lane & 63) == 63
-    first_z = (lane & 63) == 0
-
-    def body(step, carry):
-        for sub in range(width):
-            m = step * width + sub
-            for it in range(8):
-                row = 8 + 8 * it
-                value = source[m + 1, row:row + 8]
-                beside = source[m + 1, row + 1:row + 9] + source[m + 1, row - 1:row + 7]
-                lines = jnp.where(low, source[m + 2, row:row + 8], source[m, row:row + 8])
-                beside += pltpu.roll(value + lines, 64, 1)
-                beside += jnp.where(last_z, 0.0, pltpu.roll(value, 127, 1))
-                beside += jnp.where(first_z, 0.0, pltpu.roll(value, 1, 1))
-                rate = factor[m, 8 * it:8 * it + 8] - (time_step * quartic_rate) * (value * value)
-                store(m, it, value * rate + (time_step * gradient_energy) * beside)
-        return carry
-
-    lax.fori_loop(first // width, last // width, body, 0)
-
-
-def relax_kernel(half_0, half_1, mine_outer, *refs, first):
-    windows, result_hbm, (result, factor, ping, pong, metas, sems) = refs[:4], refs[-7], refs[-6:]
+    extract(tile, (window_sib,), row, column)
+
+
+def neighbour_table():
+    source = lax.broadcasted_iota(jnp.int32, (256, 128), 0) & 127
+    target = lax.broadcasted_iota(jnp.int32, (256, 128), 1)
+    beside = (jnp.abs(source - target) == 1) & ((source >> 6) == (target >> 6))
+    return jnp.where(beside, 1.0, 0.0).astype(jnp.bfloat16)
+
+
+def substep(source, factor, target, table):
+    low = lax.broadcasted_iota(jnp.int32, (8, 128), 1) < 64
+    parts = []
+    for m in range(32):
+        line = source[m + 1, 8:72]
+        upper = line.astype(jnp.bfloat16)
+        lower = (line - upper.astype(jnp.float32)).astype(jnp.bfloat16)
+        parts.append(jnp.concatenate([upper, lower], axis=1))
+    along = jnp.dot(jnp.concatenate(parts), table, preferred_element_type=jnp.float32)
+    for m in range(32):
+        for it in range(8):
+            row = 8 + 8 * it
+            value = source[m + 1, row:row + 8]
+            beside = source[m + 1, row + 1:row + 9] + source[m + 1, row - 1:row + 7]
+            lines = jnp.where(low, source[m + 2, row:row + 8], source[m, row:row + 8])
+            beside += pltpu.roll(value + lines, 64, 1) + along[64 * m + 8 * it:64 * m + 8 * it + 8]
+            rate = factor[m, 8 * it:8 * it + 8] - (time_step * quartic_rate) * (value * value)
+            target[m + 1, row:row + 8] = value * rate + (time_step * gradient_energy) * beside
+
+
+def relax_kernel(half_0, half_1, mine_outer, *refs, first, sizes):
+    result_hbm, (factor, ping, pong, metas, sems) = refs[-6], refs[-5:]
+    windows, at = [], 0
+    for size in sizes:
+        windows.append(refs[at:at + size])
+        at += size
     load_metas((half_1, mine_outer), metas, sems)
     flip = lax.axis_index("dev") & 1
     slot = inbound(metas, 0, flip) if first < 0 else 1 - inbound(metas, 0, flip)
@@ -265,39 +272,34 @@
             @pl.when(tile == first - 1 + index)
             def _(window=window, half=half, at=at):
                 def body(step, carry):
-                    for sub in range(4):
-                        m = step * 4 + sub
+                    for sub in range(8):
+                        m = step * 8 + sub
                         for it in range(4):
                             value = half[slot * HALF_BLOCKS + it * 32 + m]
                             rows = pl.multiple_of(at + 8 * it, 8)
                             ping[m + 1, pl.ds(pl.multiple_of(rows + 8, 8), 8)] = value
-                            others = window[it * 32 + m] - value * value
+                            each = 4 // len(window)
+                            others = window[it // each][it % each * 32 + m] - value * value
                             factor[m, pl.ds(rows, 8)] = base - scale * others
                     return carry
 
-                lax.fori_loop(0, 8, body, 0)
-
-    def to(buffer):
-        def store(m, it, value):
-            buffer[m + 1, 8 + 8 * it:16 + 8 * it] = value
-
-        return store
-
-    def to_result(m, it, value):
-        result[it, m] = value
-
-    substep(ping, factor, to(pong), 0, 32, 8)
-    substep(pong, factor, to(ping), 0, 32, 8)
-    substep(ping, factor, to(pong), 0, 32, 8)
+                lax.fori_loop(0, 4, body, 0)
+
+    table = neighbour_table()
+
+    def twice(step, carry):
+        substep(ping, factor, pong, table)
+        substep(pong, factor, ping, table)
+        return carry
+
+    lax.fori_loop(0, SUBSTEPS // 2, twice, 0)
     copies = []
-    for part in range(2):
-        substep(pong, factor, to_result, 16 * part, 16 * part + 16, 8)
-        lines = pl.ds(16 * part, 16)
-        copy = pltpu.make_async_copy(
-            result.at[:, lines], result_hbm.at[own_slot, :, lines], sems.at[2 + part]
-        )
+    for it in range(8):
+        copies.append(pltpu.make_async_copy(
+            ping.at[1:33, 8 + 8 * it:16 + 8 * it], result_hbm.at[own_slot, it], sems.at[2 + it]
+        ))
+    for copy in copies:
         copy.start()
-        copies.append(copy)
     for copy in copies:
         copy.wait()
 
@@ -323,9 +325,10 @@
 
     vmem = pl.BlockSpec(memory_space=pltpu.VMEM)
     anywhere = pl.BlockSpec(memory_space=pl.ANY)
-    params = pltpu.CompilerParams(vmem_limit_bytes=48 << 20)
+    params = pltpu.CompilerParams(vmem_limit_bytes=12 << 20)
     message_type = jax.ShapeDtypeStruct((2 * HALF_BLOCKS + 1, 8, 128), jnp.float32)
     tile_type = jax.ShapeDtypeStruct(TILE, jnp.float32)
+    part_type = jax.ShapeDtypeStruct((HALF_BLOCKS // 2, 8, 128), jnp.float32)
     piece_type = jax.ShapeDtypeStruct(PIECE, jnp.float32)
 
     def metas(count, sems):
@@ -364,56 +367,56 @@
     beyond = send(out_outer, sibling)
 
     tile_scratch = [pltpu.VMEM(TILE, jnp.float32)]
-    to_next, window_out_1, window_sib_1 = pl.pallas_call(
+    to_next, cross_0, cross_1, window_out_1, window_sib_1 = pl.pallas_call(
         inner_kernel,
         in_specs=[anywhere] + [vmem] * 3,
-        out_specs=[vmem] * 3,
-        out_shape=[jax.ShapeDtypeStruct((META, 8, 128), jnp.float32)] + [piece_type] * 2,
+        out_specs=[vmem] * 5,
+        out_shape=[piece_type] + [part_type] * 2 + [piece_type] * 2,
         scratch_shapes=tile_scratch + metas(3, 4),
         compiler_params=params,
         name="inner_tile",
     )(part_1, sib_outer, out_outer, beyond)
-    near = send(to_next, inward)
+    near = [send(value, inward) for value in (cross_0, cross_1, to_next)]
 
     part_0, window_out_1 = lax.optimization_barrier((part_0, window_out_1))
-    to_next, to_sib, window_out_0, window_sib_0 = pl.pallas_call(
+    to_next, to_sib_0, to_sib_1, window_out_0, window_sib_0 = pl.pallas_call(
         outer_kernel,
         in_specs=[anywhere] + [vmem] * 4,
-        out_specs=[vmem] * 4,
-        out_shape=[piece_type] * 4,
+        out_specs=[vmem] * 5,
+        out_shape=[piece_type] + [part_type] * 2 + [piece_type] * 2,
         scratch_shapes=tile_scratch + metas(4, 5),
         compiler_params=params,
         name="outer_tile",
     )(part_0, outer, sib_outer, out_outer, out_inners)
     far_out = send(to_next, inward)
-    from_sib = send(to_sib, sibling)
-    near, window_out_0 = lax.optimization_barrier((near, window_out_0))
-    near_sib = send(near[HALF_BLOCKS:], sibling)
+    from_sib = [send(value, sibling) for value in (to_sib_0, to_sib_1)]
+    *near, window_out_0 = lax.optimization_barrier((*near, window_out_0))
+    near_sib = [send(value, sibling) for value in near[:2]]
 
     def relax(name, first, halves, windows, held):
+        flat = [value for window in windows for value in window]
         return pl.pallas_call(
-            functools.partial(relax_kernel, first=first),
-            in_specs=[vmem] * 7 + [anywhere] * len(held),
+            functools.partial(relax_kernel, first=first, sizes=[len(w) for w in windows]),
+            in_specs=[vmem] * (3 + len(flat)) + [anywhere] * len(held),
             out_specs=anywhere,
             out_shape=jax.ShapeDtypeStruct((2,) + BOX_BLOCKS, jnp.float32),
             scratch_shapes=[
-                pltpu.VMEM(BOX_BLOCKS, jnp.float32),
                 pltpu.VMEM((32, 64, 128), jnp.float32),
                 pltpu.VMEM(PADDED, jnp.float32),
                 pltpu.VMEM(PADDED, jnp.float32),
-            ] + metas(2, 4),
-            input_output_aliases={7: 0} if held else {},
+            ] + metas(2, 10),
+            input_output_aliases={3 + len(flat): 0} if held else {},
             compiler_params=params,
             name=name,
-        )(*halves, outer, *windows, *held)
+        )(*halves, outer, *flat, *held)
 
     held = relax(
         "relax_sibling", 1, (sib_inner, sib_outer),
-        (window_sib_0, window_sib_1, from_sib, near_sib), (),
+        ([window_sib_0], [window_sib_1], from_sib, near_sib), (),
     )
     relaxed = relax(
         "relax_outer", -1, (out_inners, out_outer),
-        (far_out, near, window_out_0, window_out_1), (held,),
+        ([far_out], near[2:], [window_out_0], [window_out_1]), (held,),
     )
     return relaxed.transpose(0, 1, 3, 2, 4).reshape(grain_boxes.shape)
 

time: 85.6 us -> 78.3 us (0.915)
  Pallas kernels: 33.6 us -> 21.6 us
  waiting for transfers between devices: 17.1 us -> 21.2 us
  starting transfers between devices: 32.3 us -> 34.9 us
  local copies, waits for them, and re-layouts: 1.36 us -> 0 us
    pallas_call x2, Pallas kernels: 14.1 us -> 9.02 us  [relax(): pl.pallas_call(functools.partial(relax_kernel, first=first, sizes=[len(w)...]
    ppermute x9 -> x13, waiting for transfers between devices: 17.1 us -> 21.2 us  [send(): return lax.ppermute(value, 'dev', pairs)]
    pallas_call x1, Pallas kernels: 7.3 us -> 3.9 us  [on_device(): pl.pallas_call(outer_kernel, in_specs=[anywhere] + [vmem] * 4, out_specs=...]
    ppermute x9 -> x13, starting transfers between devices: 32.3 us -> 34.9 us  [send(): return lax.ppermute(value, 'dev', pairs)]
    pallas_call x1, Pallas kernels: 4.77 us -> 2.73 us  [on_device(): pl.pallas_call(local_kernel, in_specs=[vmem] * 4, out_specs=[vmem] * 2, o...]
    pallas_call x1, Pallas kernels: 5.7 us -> 4.22 us  [on_device(): pl.pallas_call(inner_kernel, in_specs=[anywhere] + [vmem] * 3, out_specs=...]
    unnamed x2 -> x0, local copies, waits for them, and re-layouts: 1.33 us -> none
  transfers between devices with their start and end apart: 9 -> 13, of which waited for: 5 -> 8; matrix products, arithmetic and copies ran while one was open for 0% -> 0% of each run, Pallas kernels for 28% -> 20%
where the time goes in v3:
time: 78.3 us; the launch traced here: 78 us
  starting transfers between devices  34.9 us (45%)
  Pallas kernels  21.6 us (28%)
  waiting for transfers between devices  21.2 us (27%)
    ppermute x13, starting transfers between devices, send(): return lax.ppermute(value, 'dev', pairs)  34.9 us
    ppermute x13, waiting for transfers between devices, send(): return lax.ppermute(value, 'dev', pairs)  21.2 us
    pallas_call x2, Pallas kernels, relax(): pl.pallas_call(functools.partial(relax_kernel, first=first, sizes=[len(w)...  9.02 us
    pallas_call x1, Pallas kernels, on_device(): pl.pallas_call(inner_kernel, in_specs=[anywhere] + [vmem] * 3, out_specs=...  4.22 us
    pallas_call x1, Pallas kernels, on_device(): pl.pallas_call(outer_kernel, in_specs=[anywhere] + [vmem] * 4, out_specs=...  3.9 us
    pallas_call x1, Pallas kernels, on_device(): pl.pallas_call(local_kernel, in_specs=[vmem] * 4, out_specs=[vmem] * 2, o...  2.73 us
    pallas_call x1, Pallas kernels, on_device(): pl.pallas_call(message_kernel, in_specs=[pl.BlockSpec(memory_space=pltpu....  1.75 us
  transfers between devices with their start and end apart: 13, of which 8 were waited for; matrix products, arithmetic and copies ran while one was open for 0% of the time, Pallas kernels for 20%

profile of v3, /device:TPU:1, one launch (start us, length us, event | category | flops | bytes accessed | tf_op | source)
XLA Modules:
  0.0 78.0 jit_solution(1233213476723824562)
XLA Ops:
  0.0 1.8 %messages.1 = (f32[257,8,128]{2,1,0:T(8,128)S(1)}, f32[257,8,128]{2,1,0:T(8,128)S(1)}) custom-call(f32[2,8,32,8,128]{4,3,2,1,0:T(8,128)} %bitcast.6, s32[2,3]{1,0:T(2,128)} %anchors_hbm.1, s32[1,2]{1,0:T(1,128)} %migrations_hbm.1), custom_call_target="tpu_custom_call" | custom-call | tf_op jit(solution)/shard_map/messages/pallas_call | solution.py:337
  1.8 1.5 %collective-permute-start = (f32[257,8,128]{2,1,0:T(8,128)S(1)}, f32[257,8,128]{2,1,0:T(8,128)S(1)}, u32[]{:S(2)}, u32[]{:S(2)}) collective-permute-start(f32[257,8,128]{2,1,0:T(8,128)S(1)} %get-tuple-element.27.mine_inner), channel_id=1, source_target_pairs={{0,1},{1,0},{2,3},{3,2},{4,5},{5,4},{6,7},{7,6},{8,9},{9,8},{10,11... | collective-permute-start | bytes 3158024 | tf_op jit(solution)/shard_map/ppermute | solution.py:322
  3.3 0.1 collective-permute-start.3
  3.4 1.7 %collective-permute-start.2 = (f32[257,8,128]{2,1,0:T(8,128)S(1)}, f32[257,8,128]{2,1,0:T(8,128)S(1)}, u32[]{:S(2)}, u32[]{:S(2)}) collective-permute-start(f32[257,8,128]{2,1,0:T(8,128)S(1)} %get-tuple-element.28.mine_outer), channel_id=1, source_target_pairs={{0,127},{1,2},{2,1},{3,4},{4,3},{5,6},{6,5},{7,8},{8,7},{9,10},{10... | collective-permute-start | bytes 3158024 | tf_op jit(solution)/shard_map/ppermute | solution.py:322
  5.0 0.5 collective-permute-done.sib_inner.half_0
  5.6 0.1 pad_maximum_fusion
  5.7 1.7 %collective-permute-start.1 = (f32[514,8,128]{2,1,0:T(8,128)S(1)}, f32[514,8,128]{2,1,0:T(8,128)S(1)}, u32[]{:S(2)}, u32[]{:S(2)}) collective-permute-start(f32[514,8,128]{2,1,0:T(8,128)S(1)} %pad_maximum_fusion), channel_id=1, source_target_pairs={{0,127},{1,2},{2,1},{3,4},{4,3},{5,6},{6,5},{7,8},{8,7},{9,10},{10... | collective-permute-start | bytes 6316040 | tf_op jit(solution)/shard_map/ppermute | solution.py:322
  7.4 0.0 collective-permute-done.3.sib_outer.half_1
  7.4 2.7 %local_tiles.1 = (f32[2,64,4,8,128]{4,3,2,1,0:T(8,128)S(1)}, f32[2,64,4,8,128]{4,3,2,1,0:T(8,128)S(1)}) custom-call(f32[257,8,128]{2,1,0:T(8,128)S(1)} %get-tuple-element.28.mine_outer, f32[257,8,128]{2,1,0:T(8,128)S(1)} %get-tuple-element.27.mine_inner, f32[257,8,128]{2,1,0:T(8,128)S(1)} %collective-permute-done.3.sib_outer.half_1, ...), custom_call_target="tpu_custom_call" | custom-call | tf_op jit(solution)/shard_map/local_tiles/pallas_call | solution.py:356
  10.1 7.8 %collective-permute-done.2.out_outer.half_1 = f32[257,8,128]{2,1,0:T(8,128)S(1)} collective-permute-done((f32[257,8,128]{2,1,0:T(8,128)S(1)}, f32[257,8,128]{2,1,0:T(8,128)S(1)}, u32[]{:S(2)}, u32[]{:S(2)}) %collective-permute-start.2) | collective-permute-done | bytes 1052704 | tf_op jit(solution)/shard_map/ppermute | solution.py:322
  17.9 6.8 %collective-permute-start.4 = (f32[257,8,128]{2,1,0:T(8,128)S(1)}, f32[257,8,128]{2,1,0:T(8,128)S(1)}, u32[]{:S(2)}, u32[]{:S(2)}) collective-permute-start(f32[257,8,128]{2,1,0:T(8,128)S(1)} %collective-permute-done.2.out_outer.half_1), channel_id=1, source_target_pairs={{0,1},{1,0},{2,3},{3,2},{4,5},{5,4},{6,7},{7,6},{8,9},{9,8},{10,11... | collective-permute-start | bytes 3158024 | tf_op jit(solution)/shard_map/ppermute | solution.py:322
  24.8 2.3 %collective-permute-done.4.beyond = f32[257,8,128]{2,1,0:T(8,128)S(1)} collective-permute-done((f32[257,8,128]{2,1,0:T(8,128)S(1)}, f32[257,8,128]{2,1,0:T(8,128)S(1)}, u32[]{:S(2)}, u32[]{:S(2)}) %collective-permute-start.4) | collective-permute-done | bytes 1052704 | tf_op jit(solution)/shard_map/ppermute | solution.py:322
  27.1 4.2 %inner_tile.1 = (f32[128,8,128]{2,1,0:T(8,128)S(1)}, f32[64,8,128]{2,1,0:T(8,128)S(1)}, f32[64,8,128]{2,1,0:T(8,128)S(1)}, f32[128,8,128]{2,1,0:T(8,128)S(1)}, f32[128,8,128]{2,1,0:T(8,128)S(1)}) custom-call(f32[2,64,4,8,128]{4,3,2,1,0:T(8,128)S(1)} %get-tuple-element.32.part, f32[257,8,128]{2,1,0:T(8,128)S(1)} %collective-permute-done.3.sib_outer.half_1, ...), custom_call_target="tpu_custom_call" | custom-call | tf_op jit(solution)/shard_map/inner_tile/pallas_call | solution.py:370
  31.3 6.4 %collective-permute-start.8 = (f32[128,8,128]{2,1,0:T(8,128)S(1)}, f32[128,8,128]{2,1,0:T(8,128)S(1)}, u32[]{:S(2)}, u32[]{:S(2)}) collective-permute-start(f32[128,8,128]{2,1,0:T(8,128)S(1)} %get-tuple-element.38), channel_id=1, source_target_pairs={{0,2},{1,127},{2,4},{3,1},{4,6},{5,3},{6,8},{7,5},{8,10},{9,7},{10... | collective-permute-start | bytes 1572872 | tf_op jit(solution)/shard_map/ppermute | solution.py:322
  37.7 0.1 collective-permute-start.6
  37.8 0.1 collective-permute-start.7
  37.9 9.0 %collective-permute-done.1.out_inners.half_0 = f32[514,8,128]{2,1,0:T(8,128)S(1)} collective-permute-done((f32[514,8,128]{2,1,0:T(8,128)S(1)}, f32[514,8,128]{2,1,0:T(8,128)S(1)}, u32[]{:S(2)}, u32[]{:S(2)}) %collective-permute-start.1) | collective-permute-done | bytes 2105376 | tf_op jit(solution)/shard_map/ppermute | solution.py:322
  46.8 3.9 %outer_tile.1 = (f32[128,8,128]{2,1,0:T(8,128)S(1)}, f32[64,8,128]{2,1,0:T(8,128)S(1)}, f32[64,8,128]{2,1,0:T(8,128)S(1)}, f32[128,8,128]{2,1,0:T(8,128)S(1)}, f32[128,8,128]{2,1,0:T(8,128)S(1)}) custom-call(f32[2,64,4,8,128]{4,3,2,1,0:T(8,128)S(1)} %get-tuple-element.34.part, f32[257,8,128]{2,1,0:T(8,128)S(1)} %get-tuple-element.28.mine_outer, ...), custom_call_target="tpu_custom_call" | custom-call | tf_op jit(solution)/shard_map/outer_tile/pallas_call | solution.py:382
  50.7 15.4 %collective-permute-start.5 = (f32[128,8,128]{2,1,0:T(8,128)S(1)}, f32[128,8,128]{2,1,0:T(8,128)S(1)}, u32[]{:S(2)}, u32[]{:S(2)}) collective-permute-start(f32[128,8,128]{2,1,0:T(8,128)S(1)} %get-tuple-element.35), channel_id=1, source_target_pairs={{0,2},{1,127},{2,4},{3,1},{4,6},{5,3},{6,8},{7,5},{8,10},{9,7},{10... | collective-permute-start | bytes 1572872 | tf_op jit(solution)/shard_map/ppermute | solution.py:322
  66.2 0.0 collective-permute-done.6
  66.2 0.0 collective-permute-done.7
  66.2 0.0 collective-permute-done.8.refs_1_
  66.2 0.1 collective-permute-start.11
  66.3 0.5 collective-permute-start.12
  66.8 0.1 collective-permute-start.10
  66.9 0.4 collective-permute-start.9
  67.3 0.5 collective-permute-done.11.refs_4_
  67.8 0.4 collective-permute-done.12.refs_5_
  68.2 0.4 collective-permute-done.10.refs_3_
  68.5 0.4 collective-permute-done.9.refs_2_
  68.9 4.5 %relax_sibling.1.refs_4_ = f32[2,8,32,8,128]{4,3,2,1,0:T(8,128)} custom-call(f32[257,8,128]{2,1,0:T(8,128)S(1)} %collective-permute-done.sib_inner.half_0, f32[257,8,128]{2,1,0:T(8,128)S(1)} %collective-permute-done.3.sib_outer.half_1, f32[257,8,128]{2,1,0:T(8,128)S(1)} %get-tuple-element.28.mine_outer, f32[128,8,128]{2,1,0:T(8,128)S(1)} %get-tuple-element.43.refs_0_, ...), custom_call_target="tpu_custom_call" | custom-call | tf_op jit(solution)/shard_map/relax_sibling/pallas_call | solution.py:398
  73.5 4.5 %relax_outer.1 = f32[2,8,32,8,128]{4,3,2,1,0:T(8,128)} custom-call(f32[514,8,128]{2,1,0:T(8,128)S(1)} %collective-permute-done.1.out_inners.half_0, f32[257,8,128]{2,1,0:T(8,128)S(1)} %collective-permute-done.2.out_outer.half_1, f32[257,8,128]{2,1,0:T(8,128)S(1)} %get-tuple-element.28.mine_outer, ...), custom_call_target="tpu_custom_call", output_to_operand_aliasing={{}: (7, {})} | custom-call | tf_op jit(solution)/shard_map/relax_outer/pallas_call | solution.py:398
  (1 shorter events, 0.0 us)
Async XLA Ops:
  1.8 3.8 %collective-permute-start = (f32[257,8,128]{2,1,0:T(8,128)S(1)}, f32[257,8,128]{2,1,0:T(8,128)S(1)}, u32[]{:S(2)}, u32[]{:S(2)}) collective-permute-start(f32[257,8,128]{2,1,0:T(8,128)S(1)} %get-tuple-element.27.mine_inner), channel_id=1, source_target_pairs={{0,1},{1,0},{2,3},{3,2},{4,5},{5,4},{6,7},{7,6},{8,9},{9,8},{10,11... | collective-permute-start | bytes 3158024 | tf_op jit(solution)/shard_map/ppermute | solution.py:322
  3.3 4.2 %collective-permute-start.3 = (f32[257,8,128]{2,1,0:T(8,128)S(1)}, f32[257,8,128]{2,1,0:T(8,128)S(1)}, u32[]{:S(2)}, u32[]{:S(2)}) collective-permute-start(f32[257,8,128]{2,1,0:T(8,128)S(1)} %get-tuple-element.28.mine_outer), channel_id=1, source_target_pairs={{0,1},{1,0},{2,3},{3,2},{4,5},{5,4},{6,7},{7,6},{8,9},{9,8},{10,11... | collective-permute-start | bytes 3158024 | tf_op jit(solution)/shard_map/ppermute | solution.py:322
  3.4 14.6 %collective-permute-start.2 = (f32[257,8,128]{2,1,0:T(8,128)S(1)}, f32[257,8,128]{2,1,0:T(8,128)S(1)}, u32[]{:S(2)}, u32[]{:S(2)}) collective-permute-start(f32[257,8,128]{2,1,0:T(8,128)S(1)} %get-tuple-element.28.mine_outer), channel_id=1, source_target_pairs={{0,127},{1,2},{2,1},{3,4},{4,3},{5,6},{6,5},{7,8},{8,7},{9,10},{10... | collective-permute-start | bytes 3158024 | tf_op jit(solution)/shard_map/ppermute | solution.py:322
  5.7 41.1 %collective-permute-start.1 = (f32[514,8,128]{2,1,0:T(8,128)S(1)}, f32[514,8,128]{2,1,0:T(8,128)S(1)}, u32[]{:S(2)}, u32[]{:S(2)}) collective-permute-start(f32[514,8,128]{2,1,0:T(8,128)S(1)} %pad_maximum_fusion), channel_id=1, source_target_pairs={{0,127},{1,2},{2,1},{3,4},{4,3},{5,6},{6,5},{7,8},{8,7},{9,10},{10... | collective-permute-start | bytes 6316040 | tf_op jit(solution)/shard_map/ppermute | solution.py:322
  17.9 9.1 %collective-permute-start.4 = (f32[257,8,128]{2,1,0:T(8,128)S(1)}, f32[257,8,128]{2,1,0:T(8,128)S(1)}, u32[]{:S(2)}, u32[]{:S(2)}) collective-permute-start(f32[257,8,128]{2,1,0:T(8,128)S(1)} %collective-permute-done.2.out_outer.half_1), channel_id=1, source_target_pairs={{0,1},{1,0},{2,3},{3,2},{4,5},{5,4},{6,7},{7,6},{8,9},{9,8},{10,11... | collective-permute-start | bytes 3158024 | tf_op jit(solution)/shard_map/ppermute | solution.py:322
  31.3 34.9 %collective-permute-start.8 = (f32[128,8,128]{2,1,0:T(8,128)S(1)}, f32[128,8,128]{2,1,0:T(8,128)S(1)}, u32[]{:S(2)}, u32[]{:S(2)}) collective-permute-start(f32[128,8,128]{2,1,0:T(8,128)S(1)} %get-tuple-element.38), channel_id=1, source_target_pairs={{0,2},{1,127},{2,4},{3,1},{4,6},{5,3},{6,8},{7,5},{8,10},{9,7},{10... | collective-permute-start | bytes 1572872 | tf_op jit(solution)/shard_map/ppermute | solution.py:322
  37.7 28.5 %collective-permute-start.6 = (f32[64,8,128]{2,1,0:T(8,128)S(1)}, f32[64,8,128]{2,1,0:T(8,128)S(1)}, u32[]{:S(2)}, u32[]{:S(2)}) collective-permute-start(f32[64,8,128]{2,1,0:T(8,128)S(1)} %get-tuple-element.36), channel_id=1, source_target_pairs={{0,2},{1,127},{2,4},{3,1},{4,6},{5,3},{6,8},{7,5},{8,10},{9,7},{10... | collective-permute-start | bytes 786440 | tf_op jit(solution)/shard_map/ppermute | solution.py:322
  37.8 28.4 %collective-permute-start.7 = (f32[64,8,128]{2,1,0:T(8,128)S(1)}, f32[64,8,128]{2,1,0:T(8,128)S(1)}, u32[]{:S(2)}, u32[]{:S(2)}) collective-permute-start(f32[64,8,128]{2,1,0:T(8,128)S(1)} %get-tuple-element.37), channel_id=1, source_target_pairs={{0,2},{1,127},{2,4},{3,1},{4,6},{5,3},{6,8},{7,5},{8,10},{9,7},{10... | collective-permute-start | bytes 786440 | tf_op jit(solution)/shard_map/ppermute | solution.py:322
  50.7 22.7 %collective-permute-start.5 = (f32[128,8,128]{2,1,0:T(8,128)S(1)}, f32[128,8,128]{2,1,0:T(8,128)S(1)}, u32[]{:S(2)}, u32[]{:S(2)}) collective-permute-start(f32[128,8,128]{2,1,0:T(8,128)S(1)} %get-tuple-element.35), channel_id=1, source_target_pairs={{0,2},{1,127},{2,4},{3,1},{4,6},{5,3},{6,8},{7,5},{8,10},{9,7},{10... | collective-permute-start | bytes 1572872 | tf_op jit(solution)/shard_map/ppermute | solution.py:322
  66.2 1.6 %collective-permute-start.11 = (f32[64,8,128]{2,1,0:T(8,128)S(1)}, f32[64,8,128]{2,1,0:T(8,128)S(1)}, u32[]{:S(2)}, u32[]{:S(2)}) collective-permute-start(f32[64,8,128]{2,1,0:T(8,128)S(1)} %collective-permute-done.6), channel_id=1, source_target_pairs={{0,1},{1,0},{2,3},{3,2},{4,5},{5,4},{6,7},{7,6},{8,9},{9,8},{10,11... | collective-permute-start | bytes 786440 | tf_op jit(solution)/shard_map/ppermute | solution.py:322
  66.3 1.9 %collective-permute-start.12 = (f32[64,8,128]{2,1,0:T(8,128)S(1)}, f32[64,8,128]{2,1,0:T(8,128)S(1)}, u32[]{:S(2)}, u32[]{:S(2)}) collective-permute-start(f32[64,8,128]{2,1,0:T(8,128)S(1)} %collective-permute-done.7), channel_id=1, source_target_pairs={{0,1},{1,0},{2,3},{3,2},{4,5},{5,4},{6,7},{7,6},{8,9},{9,8},{10,11... | collective-permute-start | bytes 786440 | tf_op jit(solution)/shard_map/ppermute | solution.py:322
  66.8 1.8 %collective-permute-start.10 = (f32[64,8,128]{2,1,0:T(8,128)S(1)}, f32[64,8,128]{2,1,0:T(8,128)S(1)}, u32[]{:S(2)}, u32[]{:S(2)}) collective-permute-start(f32[64,8,128]{2,1,0:T(8,128)S(1)} %get-tuple-element.46), channel_id=1, source_target_pairs={{0,1},{1,0},{2,3},{3,2},{4,5},{5,4},{6,7},{7,6},{8,9},{9,8},{10,11... | collective-permute-start | bytes 786440 | tf_op jit(solution)/shard_map/ppermute | solution.py:322
  66.9 2.1 %collective-permute-start.9 = (f32[64,8,128]{2,1,0:T(8,128)S(1)}, f32[64,8,128]{2,1,0:T(8,128)S(1)}, u32[]{:S(2)}, u32[]{:S(2)}) collective-permute-start(f32[64,8,128]{2,1,0:T(8,128)S(1)} %get-tuple-element.45), channel_id=1, source_target_pairs={{0,1},{1,0},{2,3},{3,2},{4,5},{5,4},{6,7},{7,6},{8,9},{9,8},{10,11... | collective-permute-start | bytes 786440 | tf_op jit(solution)/shard_map/ppermute | solution.py:322

commit v4 on v3

--- a/solution.py
+++ b/solution.py
@@ -25,12 +25,14 @@
 PADDED = (34, 80, 128)
 
 
-def load_metas(refs, metas, sems, at=META):
+def load_metas(refs, metas, sems, at=META, meanwhile=None):
     copies = [
         pltpu.make_async_copy(ref.at[META if n else at], metas.at[n], sems.at[n]) for n, ref in enumerate(refs)
     ]
     for copy in copies:
         copy.start()
+    if meanwhile is not None:
+        meanwhile()
     for copy in copies:
         copy.wait()
 
@@ -244,26 +246,42 @@
 
 
 def relax_kernel(half_0, half_1, mine_outer, *refs, first, sizes):
-    result_hbm, (factor, ping, pong, metas, sems) = refs[-6], refs[-5:]
+    last = first < 0
+    if last:
+        held, result_hbm, factor, ping, pong, metas, sems = refs[-7:]
+    else:
+        ping, factor, pong, metas, sems = refs[-5:]
     windows, at = [], 0
     for size in sizes:
         windows.append(refs[at:at + size])
         at += size
-    load_metas((half_1, mine_outer), metas, sems)
+    def edges():
+        for buffer in (ping, pong):
+            for at in (0, 33):
+                buffer[at] = jnp.zeros(PADDED[1:], jnp.float32)
+            for m in range(1, 33):
+                buffer[m, 0:8] = jnp.zeros((8, 128), jnp.float32)
+                buffer[m, 72:80] = jnp.zeros((8, 128), jnp.float32)
+
+    load_metas((half_1, mine_outer), metas, sems, meanwhile=edges)
     flip = lax.axis_index("dev") & 1
     slot = inbound(metas, 0, flip) if first < 0 else 1 - inbound(metas, 0, flip)
     own_slot = inbound(metas, 1, flip)
-    own_slot = own_slot if first < 0 else 1 - own_slot
+
+    def results(box, to, sem):
+        return [
+            pltpu.make_async_copy(
+                box.at[1:33, 8 + 8 * it:16 + 8 * it], result_hbm.at[to, it], sems.at[sem + it]
+            )
+            for it in range(8)
+        ]
+
+    copies = results(held, 1 - own_slot, 2) if last else []
+    for copy in copies:
+        copy.start()
     u, _, _ = box_meta(metas, 0, slot, flip)
     base = 1.0 + time_step * (growth_rate - 6.0 * gradient_energy)
     scale = 2.0 * coupling * time_step
-
-    for buffer in (ping, pong):
-        for at in (0, 33):
-            buffer[at] = jnp.zeros(PADDED[1:], jnp.float32)
-        for m in range(1, 33):
-            buffer[m, 0:8] = jnp.zeros((8, 128), jnp.float32)
-            buffer[m, 72:80] = jnp.zeros((8, 128), jnp.float32)
 
     for g, half in ((0, half_0), (1, half_1)):
         at = jnp.where(flip == 1, 1 - g, g) * 32
@@ -272,8 +290,8 @@
             @pl.when(tile == first - 1 + index)
             def _(window=window, half=half, at=at):
                 def body(step, carry):
-                    for sub in range(8):
-                        m = step * 8 + sub
+                    for sub in range(16):
+                        m = step * 16 + sub
                         for it in range(4):
                             value = half[slot * HALF_BLOCKS + it * 32 + m]
                             rows = pl.multiple_of(at + 8 * it, 8)
@@ -283,7 +301,7 @@
                             factor[m, pl.ds(rows, 8)] = base - scale * others
                     return carry
 
-                lax.fori_loop(0, 4, body, 0)
+                lax.fori_loop(0, 2, body, 0)
 
     table = neighbour_table()
 
@@ -293,15 +311,12 @@
         return carry
 
     lax.fori_loop(0, SUBSTEPS // 2, twice, 0)
-    copies = []
-    for it in range(8):
-        copies.append(pltpu.make_async_copy(
-            ping.at[1:33, 8 + 8 * it:16 + 8 * it], result_hbm.at[own_slot, it], sems.at[2 + it]
-        ))
-    for copy in copies:
-        copy.start()
-    for copy in copies:
-        copy.wait()
+    if last:
+        mine = results(ping, own_slot, 10)
+        for copy in mine:
+            copy.start()
+        for copy in copies + mine:
+            copy.wait()
 
 
 def on_device(grain_boxes, box_anchors, migrations):
@@ -376,7 +391,9 @@
         compiler_params=params,
         name="inner_tile",
     )(part_1, sib_outer, out_outer, beyond)
-    near = [send(value, inward) for value in (cross_0, cross_1, to_next)]
+    cross = [send(value, inward) for value in (cross_0, cross_1)]
+    to_next, out_inners = lax.optimization_barrier((to_next, out_inners))
+    near_out = send(to_next, inward)
 
     part_0, window_out_1 = lax.optimization_barrier((part_0, window_out_1))
     to_next, to_sib_0, to_sib_1, window_out_0, window_sib_0 = pl.pallas_call(
@@ -390,33 +407,30 @@
     )(part_0, outer, sib_outer, out_outer, out_inners)
     far_out = send(to_next, inward)
     from_sib = [send(value, sibling) for value in (to_sib_0, to_sib_1)]
-    *near, window_out_0 = lax.optimization_barrier((*near, window_out_0))
-    near_sib = [send(value, sibling) for value in near[:2]]
+    *cross, near_out, window_out_0 = lax.optimization_barrier((*cross, near_out, window_out_0))
+    near_sib = [send(value, sibling) for value in cross]
 
     def relax(name, first, halves, windows, held):
-        flat = [value for window in windows for value in window]
+        flat = [value for window in windows for value in window] + held
+        padded = [pltpu.VMEM(PADDED, jnp.float32)] * (1 + len(held))
+        last_type = jax.ShapeDtypeStruct((2,) + BOX_BLOCKS, jnp.float32)
         return pl.pallas_call(
             functools.partial(relax_kernel, first=first, sizes=[len(w) for w in windows]),
-            in_specs=[vmem] * (3 + len(flat)) + [anywhere] * len(held),
-            out_specs=anywhere,
-            out_shape=jax.ShapeDtypeStruct((2,) + BOX_BLOCKS, jnp.float32),
-            scratch_shapes=[
-                pltpu.VMEM((32, 64, 128), jnp.float32),
-                pltpu.VMEM(PADDED, jnp.float32),
-                pltpu.VMEM(PADDED, jnp.float32),
-            ] + metas(2, 10),
-            input_output_aliases={3 + len(flat): 0} if held else {},
+            in_specs=[vmem] * (3 + len(flat)),
+            out_specs=anywhere if held else vmem,
+            out_shape=last_type if held else jax.ShapeDtypeStruct(PADDED, jnp.float32),
+            scratch_shapes=[pltpu.VMEM((32, 64, 128), jnp.float32)] + padded + metas(2, 18),
             compiler_params=params,
             name=name,
-        )(*halves, outer, *flat, *held)
+        )(*halves, outer, *flat)
 
     held = relax(
         "relax_sibling", 1, (sib_inner, sib_outer),
-        ([window_sib_0], [window_sib_1], from_sib, near_sib), (),
+        ([window_sib_0], [window_sib_1], from_sib, near_sib), [],
     )
     relaxed = relax(
         "relax_outer", -1, (out_inners, out_outer),
-        ([far_out], near[2:], [window_out_0], [window_out_1]), (held,),
+        ([far_out], [near_out], [window_out_0], [window_out_1]), [held],
     )
     return relaxed.transpose(0, 1, 3, 2, 4).reshape(grain_boxes.shape)
 

time: 78.3 us -> 77.6 us (level)
  waiting for transfers between devices: 21.2 us -> 28.4 us
  starting transfers between devices: 34.9 us -> 29.1 us
  Pallas kernels: 21.6 us -> 19.6 us
    ppermute x13, waiting for transfers between devices: 21.2 us -> 28.4 us  [send(): return lax.ppermute(value, 'dev', pairs)]
    ppermute x13, starting transfers between devices: 34.9 us -> 29.1 us  [send(): return lax.ppermute(value, 'dev', pairs)]
    pallas_call x1, Pallas kernels: 4.22 us -> 3.41 us  [on_device(): pl.pallas_call(inner_kernel, in_specs=[anywhere] + [vmem] * 3, out_specs=...]
    pallas_call x1, Pallas kernels: 2.73 us -> 1.91 us  [on_device(): pl.pallas_call(local_kernel, in_specs=[vmem] * 4, out_specs=[vmem] * 2, o...]
  transfers between devices with their start and end apart: 13 -> 13, of which waited for: 8 -> 8; matrix products, arithmetic and copies ran while one was open for 0% -> 0% of each run, Pallas kernels for 20% -> 17%
where the time goes in v4:
time: 77.6 us; the launch traced here: 77.5 us
  starting transfers between devices  29.1 us (38%)
  waiting for transfers between devices  28.4 us (37%)
  Pallas kernels  19.6 us (25%)
    ppermute x13, starting transfers between devices, send(): return lax.ppermute(value, 'dev', pairs)  29.1 us
    ppermute x13, waiting for transfers between devices, send(): return lax.ppermute(value, 'dev', pairs)  28.4 us
    pallas_call x2, Pallas kernels, relax(): pl.pallas_call(functools.partial(relax_kernel, first=first, sizes=[len(w)...  8.24 us
    pallas_call x1, Pallas kernels, on_device(): pl.pallas_call(outer_kernel, in_specs=[anywhere] + [vmem] * 4, out_specs=...  4.31 us
    pallas_call x1, Pallas kernels, on_device(): pl.pallas_call(inner_kernel, in_specs=[anywhere] + [vmem] * 3, out_specs=...  3.41 us
    pallas_call x1, Pallas kernels, on_device(): pl.pallas_call(local_kernel, in_specs=[vmem] * 4, out_specs=[vmem] * 2, o...  1.91 us
    pallas_call x1, Pallas kernels, on_device(): pl.pallas_call(message_kernel, in_specs=[pl.BlockSpec(memory_space=pltpu....  1.75 us
  transfers between devices with their start and end apart: 13, of which 8 were waited for; matrix products, arithmetic and copies ran while one was open for 0% of the time, Pallas kernels for 17%

profile of v4, /device:TPU:1, one launch (start us, length us, event | category | flops | bytes accessed | tf_op | source)
XLA Modules:
  0.0 77.5 jit_solution(2566081460897986227)
XLA Ops:
  0.0 1.8 %messages.1 = (f32[257,8,128]{2,1,0:T(8,128)S(1)}, f32[257,8,128]{2,1,0:T(8,128)S(1)}) custom-call(f32[2,8,32,8,128]{4,3,2,1,0:T(8,128)} %bitcast.6, s32[2,3]{1,0:T(2,128)} %anchors_hbm.1, s32[1,2]{1,0:T(1,128)} %migrations_hbm.1), custom_call_target="tpu_custom_call" | custom-call | tf_op jit(solution)/shard_map/messages/pallas_call | solution.py:352
  1.8 1.5 %collective-permute-start.2 = (f32[257,8,128]{2,1,0:T(8,128)S(1)}, f32[257,8,128]{2,1,0:T(8,128)S(1)}, u32[]{:S(2)}, u32[]{:S(2)}) collective-permute-start(f32[257,8,128]{2,1,0:T(8,128)S(1)} %get-tuple-element.30.mine_inner), channel_id=1, source_target_pairs={{0,1},{1,0},{2,3},{3,2},{4,5},{5,4},{6,7},{7,6},{8,9},{9,8},{10,11... | collective-permute-start | bytes 3158024 | tf_op jit(solution)/shard_map/ppermute | solution.py:337
  3.3 0.1 collective-permute-start.1
  3.4 1.7 %collective-permute-start = (f32[257,8,128]{2,1,0:T(8,128)S(1)}, f32[257,8,128]{2,1,0:T(8,128)S(1)}, u32[]{:S(2)}, u32[]{:S(2)}) collective-permute-start(f32[257,8,128]{2,1,0:T(8,128)S(1)} %get-tuple-element.29.mine_outer), channel_id=1, source_target_pairs={{0,127},{1,2},{2,1},{3,4},{4,3},{5,6},{6,5},{7,8},{8,7},{9,10},{10... | collective-permute-start | bytes 3158024 | tf_op jit(solution)/shard_map/ppermute | solution.py:337
  5.0 0.5 collective-permute-done.2.sib_inner.half_0
  5.6 0.1 pad_maximum_fusion
  5.7 1.7 %collective-permute-start.4 = (f32[514,8,128]{2,1,0:T(8,128)S(1)}, f32[514,8,128]{2,1,0:T(8,128)S(1)}, u32[]{:S(2)}, u32[]{:S(2)}) collective-permute-start(f32[514,8,128]{2,1,0:T(8,128)S(1)} %pad_maximum_fusion), channel_id=1, source_target_pairs={{0,127},{1,2},{2,1},{3,4},{4,3},{5,6},{6,5},{7,8},{8,7},{9,10},{10... | collective-permute-start | bytes 6316040 | tf_op jit(solution)/shard_map/ppermute | solution.py:337
  7.4 0.0 collective-permute-done.1.sib_outer.half_1
  7.4 1.9 %local_tiles.1 = (f32[2,64,4,8,128]{4,3,2,1,0:T(8,128)S(1)}, f32[2,64,4,8,128]{4,3,2,1,0:T(8,128)S(1)}) custom-call(f32[257,8,128]{2,1,0:T(8,128)S(1)} %get-tuple-element.29.mine_outer, f32[257,8,128]{2,1,0:T(8,128)S(1)} %get-tuple-element.30.mine_inner, f32[257,8,128]{2,1,0:T(8,128)S(1)} %collective-permute-done.1.sib_outer.half_1, ...), custom_call_target="tpu_custom_call" | custom-call | tf_op jit(solution)/shard_map/local_tiles/pallas_call | solution.py:371
  9.3 8.6 %collective-permute-done.out_outer.half_1 = f32[257,8,128]{2,1,0:T(8,128)S(1)} collective-permute-done((f32[257,8,128]{2,1,0:T(8,128)S(1)}, f32[257,8,128]{2,1,0:T(8,128)S(1)}, u32[]{:S(2)}, u32[]{:S(2)}) %collective-permute-start) | collective-permute-done | bytes 1052704 | tf_op jit(solution)/shard_map/ppermute | solution.py:337
  17.9 6.8 %collective-permute-start.3 = (f32[257,8,128]{2,1,0:T(8,128)S(1)}, f32[257,8,128]{2,1,0:T(8,128)S(1)}, u32[]{:S(2)}, u32[]{:S(2)}) collective-permute-start(f32[257,8,128]{2,1,0:T(8,128)S(1)} %collective-permute-done.out_outer.half_1), channel_id=1, source_target_pairs={{0,1},{1,0},{2,3},{3,2},{4,5},{5,4},{6,7},{7,6},{8,9},{9,8},{10,11... | collective-permute-start | bytes 3158024 | tf_op jit(solution)/shard_map/ppermute | solution.py:337
  24.8 2.3 %collective-permute-done.3.beyond = f32[257,8,128]{2,1,0:T(8,128)S(1)} collective-permute-done((f32[257,8,128]{2,1,0:T(8,128)S(1)}, f32[257,8,128]{2,1,0:T(8,128)S(1)}, u32[]{:S(2)}, u32[]{:S(2)}) %collective-permute-start.3) | collective-permute-done | bytes 1052704 | tf_op jit(solution)/shard_map/ppermute | solution.py:337
  27.1 3.4 %inner_tile.1 = (f32[128,8,128]{2,1,0:T(8,128)S(1)}, f32[64,8,128]{2,1,0:T(8,128)S(1)}, f32[64,8,128]{2,1,0:T(8,128)S(1)}, f32[128,8,128]{2,1,0:T(8,128)S(1)}, f32[128,8,128]{2,1,0:T(8,128)S(1)}) custom-call(f32[2,64,4,8,128]{4,3,2,1,0:T(8,128)S(1)} %get-tuple-element.32.part, f32[257,8,128]{2,1,0:T(8,128)S(1)} %collective-permute-done.1.sib_outer.half_1, ...), custom_call_target="tpu_custom_call" | custom-call | tf_op jit(solution)/shard_map/inner_tile/pallas_call | solution.py:385
  30.5 10.0 %collective-permute-done.4.out_inners.half_0 = f32[514,8,128]{2,1,0:T(8,128)S(1)} collective-permute-done((f32[514,8,128]{2,1,0:T(8,128)S(1)}, f32[514,8,128]{2,1,0:T(8,128)S(1)}, u32[]{:S(2)}, u32[]{:S(2)}) %collective-permute-start.4) | collective-permute-done | bytes 2105376 | tf_op jit(solution)/shard_map/ppermute | solution.py:337
  40.5 13.6 %collective-permute-start.8 = (f32[128,8,128]{2,1,0:T(8,128)S(1)}, f32[128,8,128]{2,1,0:T(8,128)S(1)}, u32[]{:S(2)}, u32[]{:S(2)}) collective-permute-start(f32[128,8,128]{2,1,0:T(8,128)S(1)} %get-tuple-element.42), channel_id=1, source_target_pairs={{0,2},{1,127},{2,4},{3,1},{4,6},{5,3},{6,8},{7,5},{8,10},{9,7},{10... | collective-permute-start | bytes 1572872 | tf_op jit(solution)/shard_map/ppermute | solution.py:337
  54.1 0.0 collective-permute-start.6
  54.1 0.0 collective-permute-start.7
  54.2 4.3 %outer_tile.1 = (f32[128,8,128]{2,1,0:T(8,128)S(1)}, f32[64,8,128]{2,1,0:T(8,128)S(1)}, f32[64,8,128]{2,1,0:T(8,128)S(1)}, f32[128,8,128]{2,1,0:T(8,128)S(1)}, f32[128,8,128]{2,1,0:T(8,128)S(1)}) custom-call(f32[2,64,4,8,128]{4,3,2,1,0:T(8,128)S(1)} %get-tuple-element.38.part, f32[257,8,128]{2,1,0:T(8,128)S(1)} %get-tuple-element.29.mine_outer, ...), custom_call_target="tpu_custom_call" | custom-call | tf_op jit(solution)/shard_map/outer_tile/pallas_call | solution.py:399
  58.5 0.1 collective-permute-start.5
  58.6 0.1 collective-permute-start.10
  58.6 4.4 %collective-permute-done.6 = f32[64,8,128]{2,1,0:T(8,128)S(1)} collective-permute-done((f32[64,8,128]{2,1,0:T(8,128)S(1)}, f32[64,8,128]{2,1,0:T(8,128)S(1)}, u32[]{:S(2)}, u32[]{:S(2)}) %collective-permute-start.6) | collective-permute-done | bytes 262176 | tf_op jit(solution)/shard_map/ppermute | solution.py:337
  63.0 1.7 %collective-permute-start.9 = (f32[64,8,128]{2,1,0:T(8,128)S(1)}, f32[64,8,128]{2,1,0:T(8,128)S(1)}, u32[]{:S(2)}, u32[]{:S(2)}) collective-permute-start(f32[64,8,128]{2,1,0:T(8,128)S(1)} %get-tuple-element.49), channel_id=1, source_target_pairs={{0,1},{1,0},{2,3},{3,2},{4,5},{5,4},{6,7},{7,6},{8,9},{9,8},{10,11... | collective-permute-start | bytes 786440 | tf_op jit(solution)/shard_map/ppermute | solution.py:337
  64.7 1.1 %collective-permute-done.7 = f32[64,8,128]{2,1,0:T(8,128)S(1)} collective-permute-done((f32[64,8,128]{2,1,0:T(8,128)S(1)}, f32[64,8,128]{2,1,0:T(8,128)S(1)}, u32[]{:S(2)}, u32[]{:S(2)}) %collective-permute-start.7) | collective-permute-done | bytes 262176 | tf_op jit(solution)/shard_map/ppermute | solution.py:337
  65.8 0.0 collective-permute-done.8.refs_1_
  65.8 1.7 %collective-permute-start.11 = (f32[64,8,128]{2,1,0:T(8,128)S(1)}, f32[64,8,128]{2,1,0:T(8,128)S(1)}, u32[]{:S(2)}, u32[]{:S(2)}) collective-permute-start(f32[64,8,128]{2,1,0:T(8,128)S(1)} %collective-permute-done.6), channel_id=1, source_target_pairs={{0,1},{1,0},{2,3},{3,2},{4,5},{5,4},{6,7},{7,6},{8,9},{9,8},{10,11... | collective-permute-start | bytes 786440 | tf_op jit(solution)/shard_map/ppermute | solution.py:337
  67.6 0.0 collective-permute-start.12
  67.6 0.0 collective-permute-done.10.refs_3_
  67.6 1.1 %collective-permute-done.11.refs_4_ = f32[64,8,128]{2,1,0:T(8,128)S(1)} collective-permute-done((f32[64,8,128]{2,1,0:T(8,128)S(1)}, f32[64,8,128]{2,1,0:T(8,128)S(1)}, u32[]{:S(2)}, u32[]{:S(2)}) %collective-permute-start.11) | collective-permute-done | bytes 262176 | tf_op jit(solution)/shard_map/ppermute | solution.py:337
  68.7 0.4 collective-permute-done.12.refs_5_
  69.1 3.7 %relax_sibling.1.refs_4_ = f32[34,80,128]{2,1,0:T(8,128)S(1)} custom-call(f32[257,8,128]{2,1,0:T(8,128)S(1)} %collective-permute-done.2.sib_inner.half_0, f32[257,8,128]{2,1,0:T(8,128)S(1)} %collective-permute-done.1.sib_outer.half_1, f32[257,8,128]{2,1,0:T(8,128)S(1)} %get-tuple-element.29.mine_outer, f32[128,8,128]{2,1,0:T(8,128)S(1)} %get-tuple-element.47.refs_0_, ...), custom_call_target="tpu_custom_call" | custom-call | tf_op jit(solution)/shard_map/relax_sibling/pallas_call | solution.py:417
  72.8 0.0 collective-permute-done.5.refs_0_
  72.8 4.5 %relax_outer.1 = f32[2,8,32,8,128]{4,3,2,1,0:T(8,128)} custom-call(f32[514,8,128]{2,1,0:T(8,128)S(1)} %collective-permute-done.4.out_inners.half_0, f32[257,8,128]{2,1,0:T(8,128)S(1)} %collective-permute-done.out_outer.half_1, f32[257,8,128]{2,1,0:T(8,128)S(1)} %get-tuple-element.29.mine_outer, f32[128,8,128]{2,1,0:T(8,128)S(1)} %collective-permute-done.5.refs_0_, ...), custom_call_target="tpu_custom_call" | custom-call | tf_op jit(solution)/shard_map/relax_outer/pallas_call | solution.py:417
  (1 shorter events, 0.0 us)
Async XLA Ops:
  1.8 3.8 %collective-permute-start.2 = (f32[257,8,128]{2,1,0:T(8,128)S(1)}, f32[257,8,128]{2,1,0:T(8,128)S(1)}, u32[]{:S(2)}, u32[]{:S(2)}) collective-permute-start(f32[257,8,128]{2,1,0:T(8,128)S(1)} %get-tuple-element.30.mine_inner), channel_id=1, source_target_pairs={{0,1},{1,0},{2,3},{3,2},{4,5},{5,4},{6,7},{7,6},{8,9},{9,8},{10,11... | collective-permute-start | bytes 3158024 | tf_op jit(solution)/shard_map/ppermute | solution.py:337
  3.3 4.2 %collective-permute-start.1 = (f32[257,8,128]{2,1,0:T(8,128)S(1)}, f32[257,8,128]{2,1,0:T(8,128)S(1)}, u32[]{:S(2)}, u32[]{:S(2)}) collective-permute-start(f32[257,8,128]{2,1,0:T(8,128)S(1)} %get-tuple-element.29.mine_outer), channel_id=1, source_target_pairs={{0,1},{1,0},{2,3},{3,2},{4,5},{5,4},{6,7},{7,6},{8,9},{9,8},{10,11... | collective-permute-start | bytes 3158024 | tf_op jit(solution)/shard_map/ppermute | solution.py:337
  3.4 14.6 %collective-permute-start = (f32[257,8,128]{2,1,0:T(8,128)S(1)}, f32[257,8,128]{2,1,0:T(8,128)S(1)}, u32[]{:S(2)}, u32[]{:S(2)}) collective-permute-start(f32[257,8,128]{2,1,0:T(8,128)S(1)} %get-tuple-element.29.mine_outer), channel_id=1, source_target_pairs={{0,127},{1,2},{2,1},{3,4},{4,3},{5,6},{6,5},{7,8},{8,7},{9,10},{10... | collective-permute-start | bytes 3158024 | tf_op jit(solution)/shard_map/ppermute | solution.py:337
  5.7 34.8 %collective-permute-start.4 = (f32[514,8,128]{2,1,0:T(8,128)S(1)}, f32[514,8,128]{2,1,0:T(8,128)S(1)}, u32[]{:S(2)}, u32[]{:S(2)}) collective-permute-start(f32[514,8,128]{2,1,0:T(8,128)S(1)} %pad_maximum_fusion), channel_id=1, source_target_pairs={{0,127},{1,2},{2,1},{3,4},{4,3},{5,6},{6,5},{7,8},{8,7},{9,10},{10... | collective-permute-start | bytes 6316040 | tf_op jit(solution)/shard_map/ppermute | solution.py:337
  17.9 9.1 %collective-permute-start.3 = (f32[257,8,128]{2,1,0:T(8,128)S(1)}, f32[257,8,128]{2,1,0:T(8,128)S(1)}, u32[]{:S(2)}, u32[]{:S(2)}) collective-permute-start(f32[257,8,128]{2,1,0:T(8,128)S(1)} %collective-permute-done.out_outer.half_1), channel_id=1, source_target_pairs={{0,1},{1,0},{2,3},{3,2},{4,5},{5,4},{6,7},{7,6},{8,9},{9,8},{10,11... | collective-permute-start | bytes 3158024 | tf_op jit(solution)/shard_map/ppermute | solution.py:337
  40.5 25.4 %collective-permute-start.8 = (f32[128,8,128]{2,1,0:T(8,128)S(1)}, f32[128,8,128]{2,1,0:T(8,128)S(1)}, u32[]{:S(2)}, u32[]{:S(2)}) collective-permute-start(f32[128,8,128]{2,1,0:T(8,128)S(1)} %get-tuple-element.42), channel_id=1, source_target_pairs={{0,2},{1,127},{2,4},{3,1},{4,6},{5,3},{6,8},{7,5},{8,10},{9,7},{10... | collective-permute-start | bytes 1572872 | tf_op jit(solution)/shard_map/ppermute | solution.py:337
  54.1 8.9 %collective-permute-start.6 = (f32[64,8,128]{2,1,0:T(8,128)S(1)}, f32[64,8,128]{2,1,0:T(8,128)S(1)}, u32[]{:S(2)}, u32[]{:S(2)}) collective-permute-start(f32[64,8,128]{2,1,0:T(8,128)S(1)} %get-tuple-element.40), channel_id=1, source_target_pairs={{0,2},{1,127},{2,4},{3,1},{4,6},{5,3},{6,8},{7,5},{8,10},{9,7},{10... | collective-permute-start | bytes 786440 | tf_op jit(solution)/shard_map/ppermute | solution.py:337
  54.1 11.7 %collective-permute-start.7 = (f32[64,8,128]{2,1,0:T(8,128)S(1)}, f32[64,8,128]{2,1,0:T(8,128)S(1)}, u32[]{:S(2)}, u32[]{:S(2)}) collective-permute-start(f32[64,8,128]{2,1,0:T(8,128)S(1)} %get-tuple-element.41), channel_id=1, source_target_pairs={{0,2},{1,127},{2,4},{3,1},{4,6},{5,3},{6,8},{7,5},{8,10},{9,7},{10... | collective-permute-start | bytes 786440 | tf_op jit(solution)/shard_map/ppermute | solution.py:337
  58.5 14.3 %collective-permute-start.5 = (f32[128,8,128]{2,1,0:T(8,128)S(1)}, f32[128,8,128]{2,1,0:T(8,128)S(1)}, u32[]{:S(2)}, u32[]{:S(2)}) collective-permute-start(f32[128,8,128]{2,1,0:T(8,128)S(1)} %get-tuple-element.39), channel_id=1, source_target_pairs={{0,2},{1,127},{2,4},{3,1},{4,6},{5,3},{6,8},{7,5},{8,10},{9,7},{10... | collective-permute-start | bytes 1572872 | tf_op jit(solution)/shard_map/ppermute | solution.py:337
  58.6 9.0 %collective-permute-start.10 = (f32[64,8,128]{2,1,0:T(8,128)S(1)}, f32[64,8,128]{2,1,0:T(8,128)S(1)}, u32[]{:S(2)}, u32[]{:S(2)}) collective-permute-start(f32[64,8,128]{2,1,0:T(8,128)S(1)} %get-tuple-element.50), channel_id=1, source_target_pairs={{0,1},{1,0},{2,3},{3,2},{4,5},{5,4},{6,7},{7,6},{8,9},{9,8},{10,11... | collective-permute-start | bytes 786440 | tf_op jit(solution)/shard_map/ppermute | solution.py:337
  63.0 4.5 %collective-permute-start.9 = (f32[64,8,128]{2,1,0:T(8,128)S(1)}, f32[64,8,128]{2,1,0:T(8,128)S(1)}, u32[]{:S(2)}, u32[]{:S(2)}) collective-permute-start(f32[64,8,128]{2,1,0:T(8,128)S(1)} %get-tuple-element.49), channel_id=1, source_target_pairs={{0,1},{1,0},{2,3},{3,2},{4,5},{5,4},{6,7},{7,6},{8,9},{9,8},{10,11... | collective-permute-start | bytes 786440 | tf_op jit(solution)/shard_map/ppermute | solution.py:337
  65.8 2.9 %collective-permute-start.11 = (f32[64,8,128]{2,1,0:T(8,128)S(1)}, f32[64,8,128]{2,1,0:T(8,128)S(1)}, u32[]{:S(2)}, u32[]{:S(2)}) collective-permute-start(f32[64,8,128]{2,1,0:T(8,128)S(1)} %collective-permute-done.6), channel_id=1, source_target_pairs={{0,1},{1,0},{2,3},{3,2},{4,5},{5,4},{6,7},{7,6},{8,9},{9,8},{10,11... | collective-permute-start | bytes 786440 | tf_op jit(solution)/shard_map/ppermute | solution.py:337
  67.6 1.5 %collective-permute-start.12 = (f32[64,8,128]{2,1,0:T(8,128)S(1)}, f32[64,8,128]{2,1,0:T(8,128)S(1)}, u32[]{:S(2)}, u32[]{:S(2)}) collective-permute-start(f32[64,8,128]{2,1,0:T(8,128)S(1)} %collective-permute-done.7), channel_id=1, source_target_pairs={{0,1},{1,0},{2,3},{3,2},{4,5},{5,4},{6,7},{7,6},{8,9},{9,8},{10,11... | collective-permute-start | bytes 786440 | tf_op jit(solution)/shard_map/ppermute | solution.py:337

commit v5 on v4

--- a/solution.py
+++ b/solution.py
@@ -392,7 +392,6 @@
         name="inner_tile",
     )(part_1, sib_outer, out_outer, beyond)
     cross = [send(value, inward) for value in (cross_0, cross_1)]
-    to_next, out_inners = lax.optimization_barrier((to_next, out_inners))
     near_out = send(to_next, inward)
 
     part_0, window_out_1 = lax.optimization_barrier((part_0, window_out_1))

time: 77.6 us -> 77.8 us (level)
  starting transfers between devices: 29.1 us -> 36.1 us
  waiting for transfers between devices: 28.4 us -> 22.4 us
  Pallas kernels: 19.6 us -> 18.4 us
    ppermute x13, starting transfers between devices: 29.1 us -> 36.1 us  [send(): return lax.ppermute(value, 'dev', pairs)]
    ppermute x13, waiting for transfers between devices: 28.4 us -> 22.4 us  [send(): return lax.ppermute(value, 'dev', pairs)]
    pallas_call x1, Pallas kernels: 4.31 us -> 2.68 us  [on_device(): pl.pallas_call(outer_kernel, in_specs=[anywhere] + [vmem] * 4, out_specs=...]
  transfers between devices with their start and end apart: 13 -> 13, of which waited for: 8 -> 8; matrix products, arithmetic and copies ran while one was open for 0% -> 0% of each run, Pallas kernels for 17% -> 16%
where the time goes in v5:
time: 77.8 us; the launch traced here: 77.3 us
  starting transfers between devices  36.1 us (46%)
  waiting for transfers between devices  22.4 us (29%)
  Pallas kernels  18.4 us (24%)
    ppermute x13, starting transfers between devices, send(): return lax.ppermute(value, 'dev', pairs)  36.1 us
    ppermute x13, waiting for transfers between devices, send(): return lax.ppermute(value, 'dev', pairs)  22.4 us
    pallas_call x2, Pallas kernels, relax(): pl.pallas_call(functools.partial(relax_kernel, first=first, sizes=[len(w)...  8.24 us
    pallas_call x1, Pallas kernels, on_device(): pl.pallas_call(inner_kernel, in_specs=[anywhere] + [vmem] * 3, out_specs=...  3.4 us
    pallas_call x1, Pallas kernels, on_device(): pl.pallas_call(outer_kernel, in_specs=[anywhere] + [vmem] * 4, out_specs=...  2.68 us
    pallas_call x1, Pallas kernels, on_device(): pl.pallas_call(local_kernel, in_specs=[vmem] * 4, out_specs=[vmem] * 2, o...  2.32 us
    pallas_call x1, Pallas kernels, on_device(): pl.pallas_call(message_kernel, in_specs=[pl.BlockSpec(memory_space=pltpu....  1.75 us
  transfers between devices with their start and end apart: 13, of which 8 were waited for; matrix products, arithmetic and copies ran while one was open for 0% of the time, Pallas kernels for 16%

profile of v5, /device:TPU:1, one launch (start us, length us, event | category | flops | bytes accessed | tf_op | source)
XLA Modules:
  0.0 77.3 jit_solution(3338191553353479810)
XLA Ops:
  0.0 1.8 %messages.1 = (f32[257,8,128]{2,1,0:T(8,128)S(1)}, f32[257,8,128]{2,1,0:T(8,128)S(1)}) custom-call(f32[2,8,32,8,128]{4,3,2,1,0:T(8,128)} %bitcast.6, s32[2,3]{1,0:T(2,128)} %anchors_hbm.1, s32[1,2]{1,0:T(1,128)} %migrations_hbm.1), custom_call_target="tpu_custom_call" | custom-call | tf_op jit(solution)/shard_map/messages/pallas_call | solution.py:352
  1.8 1.5 %collective-permute-start = (f32[257,8,128]{2,1,0:T(8,128)S(1)}, f32[257,8,128]{2,1,0:T(8,128)S(1)}, u32[]{:S(2)}, u32[]{:S(2)}) collective-permute-start(f32[257,8,128]{2,1,0:T(8,128)S(1)} %get-tuple-element.27.mine_inner), channel_id=1, source_target_pairs={{0,1},{1,0},{2,3},{3,2},{4,5},{5,4},{6,7},{7,6},{8,9},{9,8},{10,11... | collective-permute-start | bytes 3158024 | tf_op jit(solution)/shard_map/ppermute | solution.py:337
  3.3 0.1 collective-permute-start.3
  3.4 1.7 %collective-permute-start.2 = (f32[257,8,128]{2,1,0:T(8,128)S(1)}, f32[257,8,128]{2,1,0:T(8,128)S(1)}, u32[]{:S(2)}, u32[]{:S(2)}) collective-permute-start(f32[257,8,128]{2,1,0:T(8,128)S(1)} %get-tuple-element.28.mine_outer), channel_id=1, source_target_pairs={{0,127},{1,2},{2,1},{3,4},{4,3},{5,6},{6,5},{7,8},{8,7},{9,10},{10... | collective-permute-start | bytes 3158024 | tf_op jit(solution)/shard_map/ppermute | solution.py:337
  5.0 0.5 collective-permute-done.sib_inner.half_0
  5.6 0.1 pad_maximum_fusion
  5.7 1.7 %collective-permute-start.1 = (f32[514,8,128]{2,1,0:T(8,128)S(1)}, f32[514,8,128]{2,1,0:T(8,128)S(1)}, u32[]{:S(2)}, u32[]{:S(2)}) collective-permute-start(f32[514,8,128]{2,1,0:T(8,128)S(1)} %pad_maximum_fusion), channel_id=1, source_target_pairs={{0,127},{1,2},{2,1},{3,4},{4,3},{5,6},{6,5},{7,8},{8,7},{9,10},{10... | collective-permute-start | bytes 6316040 | tf_op jit(solution)/shard_map/ppermute | solution.py:337
  7.4 0.0 collective-permute-done.3.sib_outer.half_1
  7.4 2.3 %local_tiles.1 = (f32[2,64,4,8,128]{4,3,2,1,0:T(8,128)S(1)}, f32[2,64,4,8,128]{4,3,2,1,0:T(8,128)S(1)}) custom-call(f32[257,8,128]{2,1,0:T(8,128)S(1)} %get-tuple-element.28.mine_outer, f32[257,8,128]{2,1,0:T(8,128)S(1)} %get-tuple-element.27.mine_inner, f32[257,8,128]{2,1,0:T(8,128)S(1)} %collective-permute-done.3.sib_outer.half_1, ...), custom_call_target="tpu_custom_call" | custom-call | tf_op jit(solution)/shard_map/local_tiles/pallas_call | solution.py:371
  9.7 8.2 %collective-permute-done.2.out_outer.half_1 = f32[257,8,128]{2,1,0:T(8,128)S(1)} collective-permute-done((f32[257,8,128]{2,1,0:T(8,128)S(1)}, f32[257,8,128]{2,1,0:T(8,128)S(1)}, u32[]{:S(2)}, u32[]{:S(2)}) %collective-permute-start.2) | collective-permute-done | bytes 1052704 | tf_op jit(solution)/shard_map/ppermute | solution.py:337
  17.9 6.8 %collective-permute-start.4 = (f32[257,8,128]{2,1,0:T(8,128)S(1)}, f32[257,8,128]{2,1,0:T(8,128)S(1)}, u32[]{:S(2)}, u32[]{:S(2)}) collective-permute-start(f32[257,8,128]{2,1,0:T(8,128)S(1)} %collective-permute-done.2.out_outer.half_1), channel_id=1, source_target_pairs={{0,1},{1,0},{2,3},{3,2},{4,5},{5,4},{6,7},{7,6},{8,9},{9,8},{10,11... | collective-permute-start | bytes 3158024 | tf_op jit(solution)/shard_map/ppermute | solution.py:337
  24.8 2.3 %collective-permute-done.4.beyond = f32[257,8,128]{2,1,0:T(8,128)S(1)} collective-permute-done((f32[257,8,128]{2,1,0:T(8,128)S(1)}, f32[257,8,128]{2,1,0:T(8,128)S(1)}, u32[]{:S(2)}, u32[]{:S(2)}) %collective-permute-start.4) | collective-permute-done | bytes 1052704 | tf_op jit(solution)/shard_map/ppermute | solution.py:337
  27.1 3.4 %inner_tile.1 = (f32[128,8,128]{2,1,0:T(8,128)S(1)}, f32[64,8,128]{2,1,0:T(8,128)S(1)}, f32[64,8,128]{2,1,0:T(8,128)S(1)}, f32[128,8,128]{2,1,0:T(8,128)S(1)}, f32[128,8,128]{2,1,0:T(8,128)S(1)}) custom-call(f32[2,64,4,8,128]{4,3,2,1,0:T(8,128)S(1)} %get-tuple-element.32.part, f32[257,8,128]{2,1,0:T(8,128)S(1)} %collective-permute-done.3.sib_outer.half_1, ...), custom_call_target="tpu_custom_call" | custom-call | tf_op jit(solution)/shard_map/inner_tile/pallas_call | solution.py:385
  30.5 7.2 %collective-permute-start.8 = (f32[128,8,128]{2,1,0:T(8,128)S(1)}, f32[128,8,128]{2,1,0:T(8,128)S(1)}, u32[]{:S(2)}, u32[]{:S(2)}) collective-permute-start(f32[128,8,128]{2,1,0:T(8,128)S(1)} %get-tuple-element.38), channel_id=1, source_target_pairs={{0,2},{1,127},{2,4},{3,1},{4,6},{5,3},{6,8},{7,5},{8,10},{9,7},{10... | collective-permute-start | bytes 1572872 | tf_op jit(solution)/shard_map/ppermute | solution.py:337
  37.7 0.1 collective-permute-start.6
  37.8 0.1 collective-permute-start.7
  37.9 9.8 %collective-permute-done.1.out_inners.half_0 = f32[514,8,128]{2,1,0:T(8,128)S(1)} collective-permute-done((f32[514,8,128]{2,1,0:T(8,128)S(1)}, f32[514,8,128]{2,1,0:T(8,128)S(1)}, u32[]{:S(2)}, u32[]{:S(2)}) %collective-permute-start.1) | collective-permute-done | bytes 2105376 | tf_op jit(solution)/shard_map/ppermute | solution.py:337
  47.6 2.7 %outer_tile.1 = (f32[128,8,128]{2,1,0:T(8,128)S(1)}, f32[64,8,128]{2,1,0:T(8,128)S(1)}, f32[64,8,128]{2,1,0:T(8,128)S(1)}, f32[128,8,128]{2,1,0:T(8,128)S(1)}, f32[128,8,128]{2,1,0:T(8,128)S(1)}) custom-call(f32[2,64,4,8,128]{4,3,2,1,0:T(8,128)S(1)} %get-tuple-element.34.part, f32[257,8,128]{2,1,0:T(8,128)S(1)} %get-tuple-element.28.mine_outer, ...), custom_call_target="tpu_custom_call" | custom-call | tf_op jit(solution)/shard_map/outer_tile/pallas_call | solution.py:398
  50.3 15.8 %collective-permute-start.5 = (f32[128,8,128]{2,1,0:T(8,128)S(1)}, f32[128,8,128]{2,1,0:T(8,128)S(1)}, u32[]{:S(2)}, u32[]{:S(2)}) collective-permute-start(f32[128,8,128]{2,1,0:T(8,128)S(1)} %get-tuple-element.35), channel_id=1, source_target_pairs={{0,2},{1,127},{2,4},{3,1},{4,6},{5,3},{6,8},{7,5},{8,10},{9,7},{10... | collective-permute-start | bytes 1572872 | tf_op jit(solution)/shard_map/ppermute | solution.py:337
  66.2 0.0 collective-permute-done.6
  66.2 0.0 collective-permute-done.7
  66.2 0.1 collective-permute-start.11
  66.3 0.5 collective-permute-start.12
  66.8 0.1 collective-permute-start.10
  66.9 0.4 collective-permute-start.9
  67.3 0.5 collective-permute-done.11.refs_4_
  67.8 0.4 collective-permute-done.12.refs_5_
  68.2 0.4 collective-permute-done.10.refs_3_
  68.5 0.4 collective-permute-done.9.refs_2_
  68.9 3.7 %relax_sibling.1.refs_4_ = f32[34,80,128]{2,1,0:T(8,128)S(1)} custom-call(f32[257,8,128]{2,1,0:T(8,128)S(1)} %collective-permute-done.sib_inner.half_0, f32[257,8,128]{2,1,0:T(8,128)S(1)} %collective-permute-done.3.sib_outer.half_1, f32[257,8,128]{2,1,0:T(8,128)S(1)} %get-tuple-element.28.mine_outer, f32[128,8,128]{2,1,0:T(8,128)S(1)} %get-tuple-element.43.refs_0_, ...), custom_call_target="tpu_custom_call" | custom-call | tf_op jit(solution)/shard_map/relax_sibling/pallas_call | solution.py:416
  72.6 0.0 collective-permute-done.5.refs_0_
  72.6 4.5 %relax_outer.1 = f32[2,8,32,8,128]{4,3,2,1,0:T(8,128)} custom-call(f32[514,8,128]{2,1,0:T(8,128)S(1)} %collective-permute-done.1.out_inners.half_0, f32[257,8,128]{2,1,0:T(8,128)S(1)} %collective-permute-done.2.out_outer.half_1, f32[257,8,128]{2,1,0:T(8,128)S(1)} %get-tuple-element.28.mine_outer, f32[128,8,128]{2,1,0:T(8,128)S(1)} %collective-permute-done.5.refs_0_, ...), custom_call_target="tpu_custom_call" | custom-call | tf_op jit(solution)/shard_map/relax_outer/pallas_call | solution.py:416
  (1 shorter events, 0.0 us)
Async XLA Ops:
  1.8 3.8 %collective-permute-start = (f32[257,8,128]{2,1,0:T(8,128)S(1)}, f32[257,8,128]{2,1,0:T(8,128)S(1)}, u32[]{:S(2)}, u32[]{:S(2)}) collective-permute-start(f32[257,8,128]{2,1,0:T(8,128)S(1)} %get-tuple-element.27.mine_inner), channel_id=1, source_target_pairs={{0,1},{1,0},{2,3},{3,2},{4,5},{5,4},{6,7},{7,6},{8,9},{9,8},{10,11... | collective-permute-start | bytes 3158024 | tf_op jit(solution)/shard_map/ppermute | solution.py:337
  3.3 4.2 %collective-permute-start.3 = (f32[257,8,128]{2,1,0:T(8,128)S(1)}, f32[257,8,128]{2,1,0:T(8,128)S(1)}, u32[]{:S(2)}, u32[]{:S(2)}) collective-permute-start(f32[257,8,128]{2,1,0:T(8,128)S(1)} %get-tuple-element.28.mine_outer), channel_id=1, source_target_pairs={{0,1},{1,0},{2,3},{3,2},{4,5},{5,4},{6,7},{7,6},{8,9},{9,8},{10,11... | collective-permute-start | bytes 3158024 | tf_op jit(solution)/shard_map/ppermute | solution.py:337
  3.4 14.6 %collective-permute-start.2 = (f32[257,8,128]{2,1,0:T(8,128)S(1)}, f32[257,8,128]{2,1,0:T(8,128)S(1)}, u32[]{:S(2)}, u32[]{:S(2)}) collective-permute-start(f32[257,8,128]{2,1,0:T(8,128)S(1)} %get-tuple-element.28.mine_outer), channel_id=1, source_target_pairs={{0,127},{1,2},{2,1},{3,4},{4,3},{5,6},{6,5},{7,8},{8,7},{9,10},{10... | collective-permute-start | bytes 3158024 | tf_op jit(solution)/shard_map/ppermute | solution.py:337
  5.7 41.9 %collective-permute-start.1 = (f32[514,8,128]{2,1,0:T(8,128)S(1)}, f32[514,8,128]{2,1,0:T(8,128)S(1)}, u32[]{:S(2)}, u32[]{:S(2)}) collective-permute-start(f32[514,8,128]{2,1,0:T(8,128)S(1)} %pad_maximum_fusion), channel_id=1, source_target_pairs={{0,127},{1,2},{2,1},{3,4},{4,3},{5,6},{6,5},{7,8},{8,7},{9,10},{10... | collective-permute-start | bytes 6316040 | tf_op jit(solution)/shard_map/ppermute | solution.py:337
  17.9 9.1 %collective-permute-start.4 = (f32[257,8,128]{2,1,0:T(8,128)S(1)}, f32[257,8,128]{2,1,0:T(8,128)S(1)}, u32[]{:S(2)}, u32[]{:S(2)}) collective-permute-start(f32[257,8,128]{2,1,0:T(8,128)S(1)} %collective-permute-done.2.out_outer.half_1), channel_id=1, source_target_pairs={{0,1},{1,0},{2,3},{3,2},{4,5},{5,4},{6,7},{7,6},{8,9},{9,8},{10,11... | collective-permute-start | bytes 3158024 | tf_op jit(solution)/shard_map/ppermute | solution.py:337
  30.5 35.7 %collective-permute-start.8 = (f32[128,8,128]{2,1,0:T(8,128)S(1)}, f32[128,8,128]{2,1,0:T(8,128)S(1)}, u32[]{:S(2)}, u32[]{:S(2)}) collective-permute-start(f32[128,8,128]{2,1,0:T(8,128)S(1)} %get-tuple-element.38), channel_id=1, source_target_pairs={{0,2},{1,127},{2,4},{3,1},{4,6},{5,3},{6,8},{7,5},{8,10},{9,7},{10... | collective-permute-start | bytes 1572872 | tf_op jit(solution)/shard_map/ppermute | solution.py:337
  37.7 28.5 %collective-permute-start.6 = (f32[64,8,128]{2,1,0:T(8,128)S(1)}, f32[64,8,128]{2,1,0:T(8,128)S(1)}, u32[]{:S(2)}, u32[]{:S(2)}) collective-permute-start(f32[64,8,128]{2,1,0:T(8,128)S(1)} %get-tuple-element.36), channel_id=1, source_target_pairs={{0,2},{1,127},{2,4},{3,1},{4,6},{5,3},{6,8},{7,5},{8,10},{9,7},{10... | collective-permute-start | bytes 786440 | tf_op jit(solution)/shard_map/ppermute | solution.py:337
  37.8 28.4 %collective-permute-start.7 = (f32[64,8,128]{2,1,0:T(8,128)S(1)}, f32[64,8,128]{2,1,0:T(8,128)S(1)}, u32[]{:S(2)}, u32[]{:S(2)}) collective-permute-start(f32[64,8,128]{2,1,0:T(8,128)S(1)} %get-tuple-element.37), channel_id=1, source_target_pairs={{0,2},{1,127},{2,4},{3,1},{4,6},{5,3},{6,8},{7,5},{8,10},{9,7},{10... | collective-permute-start | bytes 786440 | tf_op jit(solution)/shard_map/ppermute | solution.py:337
  50.3 22.3 %collective-permute-start.5 = (f32[128,8,128]{2,1,0:T(8,128)S(1)}, f32[128,8,128]{2,1,0:T(8,128)S(1)}, u32[]{:S(2)}, u32[]{:S(2)}) collective-permute-start(f32[128,8,128]{2,1,0:T(8,128)S(1)} %get-tuple-element.35), channel_id=1, source_target_pairs={{0,2},{1,127},{2,4},{3,1},{4,6},{5,3},{6,8},{7,5},{8,10},{9,7},{10... | collective-permute-start | bytes 1572872 | tf_op jit(solution)/shard_map/ppermute | solution.py:337
  66.2 1.6 %collective-permute-start.11 = (f32[64,8,128]{2,1,0:T(8,128)S(1)}, f32[64,8,128]{2,1,0:T(8,128)S(1)}, u32[]{:S(2)}, u32[]{:S(2)}) collective-permute-start(f32[64,8,128]{2,1,0:T(8,128)S(1)} %collective-permute-done.6), channel_id=1, source_target_pairs={{0,1},{1,0},{2,3},{3,2},{4,5},{5,4},{6,7},{7,6},{8,9},{9,8},{10,11... | collective-permute-start | bytes 786440 | tf_op jit(solution)/shard_map/ppermute | solution.py:337
  66.3 1.9 %collective-permute-start.12 = (f32[64,8,128]{2,1,0:T(8,128)S(1)}, f32[64,8,128]{2,1,0:T(8,128)S(1)}, u32[]{:S(2)}, u32[]{:S(2)}) collective-permute-start(f32[64,8,128]{2,1,0:T(8,128)S(1)} %collective-permute-done.7), channel_id=1, source_target_pairs={{0,1},{1,0},{2,3},{3,2},{4,5},{5,4},{6,7},{7,6},{8,9},{9,8},{10,11... | collective-permute-start | bytes 786440 | tf_op jit(solution)/shard_map/ppermute | solution.py:337
  66.8 1.8 %collective-permute-start.10 = (f32[64,8,128]{2,1,0:T(8,128)S(1)}, f32[64,8,128]{2,1,0:T(8,128)S(1)}, u32[]{:S(2)}, u32[]{:S(2)}) collective-permute-start(f32[64,8,128]{2,1,0:T(8,128)S(1)} %get-tuple-element.46), channel_id=1, source_target_pairs={{0,1},{1,0},{2,3},{3,2},{4,5},{5,4},{6,7},{7,6},{8,9},{9,8},{10,11... | collective-permute-start | bytes 786440 | tf_op jit(solution)/shard_map/ppermute | solution.py:337
  66.9 2.1 %collective-permute-start.9 = (f32[64,8,128]{2,1,0:T(8,128)S(1)}, f32[64,8,128]{2,1,0:T(8,128)S(1)}, u32[]{:S(2)}, u32[]{:S(2)}) collective-permute-start(f32[64,8,128]{2,1,0:T(8,128)S(1)} %get-tuple-element.45), channel_id=1, source_target_pairs={{0,1},{1,0},{2,3},{3,2},{4,5},{5,4},{6,7},{7,6},{8,9},{9,8},{10,11... | collective-permute-start | bytes 786440 | tf_op jit(solution)/shard_map/ppermute | solution.py:337
